TPU v7x, 256 devices: a whole 4x4x8 slice. The times are simulated.
256 devices in a mesh: seq: 64 (over x, z, core), ch: 4 (over y).
Axes of the slice: x: 4, y: 4, z: 8, core: 2. Of those that a mesh axis runs over, the one named last changes fastest.
Arguments:
- proj: bfloat16 [3, 128, 65536], P(None, 'ch', 'seq'), may hold values from -6 to 6
- cotangent: bfloat16 [128, 65536], P('ch', 'seq'), may hold values from -6 to 6
- short_w: float32 [3, 128, 3], P(None, 'ch'), may hold values from -3.5 to 3.5
- filter_in: float32 [32, 64], replicated, may hold values from -5 to 5
- filter_out: float32 [64, 128], P(None, 'ch'), may hold values from -0.75 to 0.75
- rates: float32 [128], P('ch'), may hold values from 0.25 to 2184
Outputs:
- grad_proj: bfloat16 [3, 128, 65536], P(None, 'ch', 'seq')
- grad_short: float32 [3, 128, 3], P(None, 'ch')
- grad_filter_out: float32 [64, 128], P(None, 'ch')
- grad_filter_in: float32 [32, 64], replicated
All inputs are finite; a program needn't handle non-finite values.
Results may differ from a plain program's by a relative error of at most 0.0013.
Values may be sent and summed in bfloat16 or wider, within the bound.
A program may use at most 64 MiB of HBM per device.

v0:
```python
import math

import jax
import jax.numpy as jnp
from jax import lax
from jax.sharding import PartitionSpec as P

PRECISE = lax.Precision.HIGHEST


def shifted(value, axis, by):
    length = lax.axis_size(axis)
    pairs = [(i, i + by) for i in range(length) if 0 <= i + by < length]
    return lax.ppermute(value, axis, pairs)


def position_features(positions, length, feature_count):
    feature_index = jnp.arange(feature_count, dtype=jnp.int32)
    multiplier = (1 + feature_index // 2 * 499) % length
    upper = positions // 1024
    lower = positions % 1024
    phases = (
        upper[:, None] * (multiplier * 1024 % length)[None, :]
        + lower[:, None] * multiplier[None, :]
    ) % length
    angles = phases.astype(jnp.float32) * (2.0 * math.pi / length)
    return jnp.where((feature_index % 2 == 0)[None, :], jnp.cos(angles), jnp.sin(angles))


def angle_tables(row_count, col_count, row_start, col_start, modulus):
    row_index = row_start + jnp.arange(row_count, dtype=jnp.int32)
    col_index = col_start + jnp.arange(col_count, dtype=jnp.int32)
    phases = row_index[:, None] * col_index[None, :] % modulus
    angles = phases.astype(jnp.float32) * (2.0 * math.pi / modulus)
    return (jnp.cos(angles), jnp.sin(angles))


def rotate(real_part, imag_part, cosine, sine, sign):
    return (
        real_part * cosine - sign * imag_part * sine,
        imag_part * cosine + sign * real_part * sine,
    )


def dft_axis(real_part, imag_part, form, cosine, sine, sign):
    real_cos = jnp.einsum(form, real_part, cosine, precision=PRECISE)
    real_sin = jnp.einsum(form, real_part, sine, precision=PRECISE)
    imag_cos = jnp.einsum(form, imag_part, cosine, precision=PRECISE)
    imag_sin = jnp.einsum(form, imag_part, sine, precision=PRECISE)
    return (real_cos - sign * imag_sin, imag_cos + sign * real_sin)


def shards(proj, cotangent, short_w, filter_in, filter_out, rates):
    tap_count = short_w.shape[2]
    channels = proj.shape[1]
    devices = lax.axis_size("seq")
    tokens_here = proj.shape[2]
    length = devices * tokens_here
    modulus = 2 * length
    norm_scale = 1.0 / math.sqrt(length)
    column_width = tokens_here // devices
    first_split = math.gcd(tokens_here, 64)
    second_split = tokens_here // first_split
    device_index = lax.axis_index("seq")
    rim_cols = shifted(proj[:, :, tokens_here - (tap_count - 1) :], "seq", 1)
    extended = jnp.concatenate([rim_cols, proj], 2).astype(jnp.float32)

    def delayed(offset):
        return extended[:, :, tap_count - 1 - offset : tap_count - 1 - offset + tokens_here]

    mixed_all = short_w[:, :, 0, None] * delayed(0)
    for offset in range(1, tap_count):
        mixed_all = mixed_all + short_w[:, :, offset, None] * delayed(offset)
    query_part, key_part, value_part = (mixed_all[0], mixed_all[1], mixed_all[2])
    gated_prod = key_part * value_part
    cotangent_full = cotangent.astype(jnp.float32)
    grad_conv = cotangent_full * query_part
    both_signals = jnp.concatenate([gated_prod, grad_conv], 0).reshape(2 * channels, 1, tokens_here)
    columns = lax.all_to_all(both_signals, "seq", split_axis=2, concat_axis=1, tiled=True)
    block_start = jnp.arange(devices, dtype=jnp.int32) * tokens_here
    offset_start = device_index * column_width + jnp.arange(column_width, dtype=jnp.int32)
    column_pos = (block_start[:, None] + offset_start[None, :]).reshape(devices * column_width)
    features = position_features(column_pos, length, filter_in.shape[0])
    preact = jnp.dot(features, filter_in, precision=PRECISE, preferred_element_type=jnp.float32)
    hidden = jnp.sin(preact)
    modulated = jnp.einsum("to,oc->ct", hidden, filter_out, precision=PRECISE)
    relative = column_pos.astype(jnp.float32) / length
    spread = jnp.sqrt(jnp.expm1(-2.0 * rates) / jnp.expm1(-2.0 * rates / length))
    envelope = jnp.exp(-rates[:, None] * relative[None, :]) / spread[:, None]
    kernel = (envelope * modulated).reshape(channels, devices, column_width)
    stacked = jnp.concatenate([columns[:channels], kernel, columns[channels:]], 0)
    cos_outer, sin_outer = angle_tables(devices, 2 * devices, 0, 0, 2 * devices)
    turned_real = jnp.einsum("ran,ak->rkn", stacked, cos_outer, precision=PRECISE)
    turned_imag = -jnp.einsum("ran,ak->rkn", stacked, sin_outer, precision=PRECISE)
    cos_turn, sin_turn = angle_tables(
        2 * devices, column_width, 0, device_index * column_width, modulus
    )
    turned_real, turned_imag = rotate(turned_real, turned_imag, cos_turn, sin_turn, -1.0)
    moved_real, moved_imag = (
        lax.all_to_all(turned_real, "seq", split_axis=1, concat_axis=2, tiled=True),
        lax.all_to_all(turned_imag, "seq", split_axis=1, concat_axis=2, tiled=True),
    )
    row_total = moved_real.shape[0]
    cos_first, sin_first = angle_tables(first_split, first_split, 0, 0, first_split)
    cos_second, sin_second = angle_tables(second_split, second_split, 0, 0, second_split)
    cos_mid, sin_mid = angle_tables(first_split, second_split, 0, 0, tokens_here)
    grid_real = moved_real.reshape(row_total, 2, first_split, second_split)
    grid_imag = moved_imag.reshape(row_total, 2, first_split, second_split)
    grid_real, grid_imag = dft_axis(
        grid_real, grid_imag, "rkab,ac->rkcb", cos_first, sin_first, -1.0
    )
    grid_real, grid_imag = rotate(grid_real, grid_imag, cos_mid, sin_mid, -1.0)
    spec_real, spec_imag = dft_axis(
        grid_real, grid_imag, "rkcb,bd->rkcd", cos_second, sin_second, -1.0
    )
    gated_real, gated_imag = (spec_real[:channels], spec_imag[:channels])
    kernel_real, kernel_imag = (
        spec_real[channels : 2 * channels],
        spec_imag[channels : 2 * channels],
    )
    grad_real, grad_imag = (spec_real[2 * channels :], spec_imag[2 * channels :])
    conv_real = gated_real * kernel_real - gated_imag * kernel_imag
    conv_imag = gated_real * kernel_imag + gated_imag * kernel_real
    back_real = grad_real * kernel_real + grad_imag * kernel_imag
    back_imag = grad_imag * kernel_real - grad_real * kernel_imag
    kgrad_real = grad_real * gated_real + grad_imag * gated_imag
    kgrad_imag = grad_imag * gated_real - grad_real * gated_imag
    cos_back, sin_back = angle_tables(2, tokens_here, 2 * device_index, 0, modulus)
    cos_last, sin_last = angle_tables(2 * devices, devices, 0, 0, 2 * devices)
    real_part = jnp.concatenate([conv_real, back_real, kgrad_real], 0)
    rows = real_part.shape[0]
    part_real, part_imag = dft_axis(
        real_part,
        jnp.concatenate([conv_imag, back_imag, kgrad_imag], 0),
        "rkcd,db->rkcb",
        cos_second,
        sin_second,
        1.0,
    )
    part_real, part_imag = rotate(part_real, part_imag, cos_mid, sin_mid, 1.0)
    part_real, part_imag = dft_axis(
        part_real, part_imag, "rkcb,ca->rkab", cos_first, sin_first, 1.0
    )
    part_real = part_real.reshape(rows, 2, tokens_here)
    part_imag = part_imag.reshape(rows, 2, tokens_here)
    part_real, part_imag = rotate(part_real, part_imag, cos_back[None], sin_back[None], 1.0)
    spread_real = lax.all_to_all(part_real, "seq", split_axis=2, concat_axis=1, tiled=True)
    spread_imag = lax.all_to_all(part_imag, "seq", split_axis=2, concat_axis=1, tiled=True)
    real_out = jnp.einsum("rkn,ka->ran", spread_real, cos_last, precision=PRECISE)
    real_out = (real_out - jnp.einsum("rkn,ka->ran", spread_imag, sin_last, precision=PRECISE)) * (
        1.0 / modulus
    )
    conv_cols = real_out[:channels]
    gated_cols = real_out[channels : 2 * channels]
    kernel_grad = real_out[2 * channels :]
    returned = lax.all_to_all(
        jnp.concatenate([conv_cols, gated_cols], 0), "seq", split_axis=1, concat_axis=2, tiled=True
    )
    returned = returned.reshape(2 * channels, tokens_here)
    conv_out = returned[:channels]
    grad_gated = returned[channels:]
    grad_mixed = jnp.stack(
        [cotangent_full * conv_out, grad_gated * value_part, grad_gated * key_part]
    )
    short_part = jnp.stack(
        [jnp.sum(grad_mixed * delayed(offset), axis=2) for offset in range(tap_count)], axis=2
    )
    weighted = envelope * kernel_grad.reshape(channels, devices * column_width)
    out_part = jnp.einsum("to,ct->oc", hidden, weighted, precision=PRECISE)
    grad_hidden = jnp.einsum("ct,oc->to", weighted, filter_out, precision=PRECISE)
    in_part = jnp.einsum("tf,to->fo", features, grad_hidden * jnp.cos(preact), precision=PRECISE)
    next_rim = shifted(grad_mixed[:, :, : tap_count - 1], "seq", -1)
    grad_extended = jnp.concatenate([grad_mixed, next_rim], 2)
    result = short_w[:, :, 0, None] * grad_extended[:, :, 0:tokens_here]
    for offset in range(1, tap_count):
        result = (
            result
            + short_w[:, :, offset, None] * grad_extended[:, :, offset : offset + tokens_here]
        )
    grad_proj = result.astype(jnp.bfloat16)
    short_total, out_total = lax.psum((short_part, out_part), "seq")
    in_total = lax.psum(in_part, ("seq", "ch"))
    return (grad_proj, short_total * norm_scale, out_total * norm_scale, in_total * norm_scale)


def solution(mesh):
    placed = (
        P(None, "ch", "seq"),
        P("ch", "seq"),
        P(None, "ch", None),
        P(),
        P(None, "ch"),
        P("ch"),
    )
    return jax.shard_map(
        shards,
        mesh=mesh,
        in_specs=placed,
        out_specs=(P(None, "ch", "seq"), P(None, "ch", None), P(None, "ch"), P()),
        check_vma=False,
    )
```

profile of v0, /device:TPU:1, one launch (start us, length us, event | category | flops | bytes accessed | tf_op | source)
XLA Modules:
  0.0 594.5 jit_solution(10087766709720511439)
XLA Ops:
  1.5 4.9 collective-permute-start
  7.5 5.1 fusion.244
  15.6 3.8 reduce
  21.5 11.3 %all-to-all-start = ((f32[64,1,1024]{2,1,0:T(1,128)}), f32[64,1,1024]{2,1,0:T(1,128)}, u32[]{:S(2)}, u32[]{:S(2)}) async-start(f32[64,1,1024]{2,1,0:T(1,128)} %reshape.320), calls=%async_computation | async-start | bytes 524288 | tf_op jit(solution)/shard_map/all_to_all | solution.py:79
  38.8 5.7 all-to-all-done
  44.5 2.9 reduce.1
  47.4 2.4 reshape.321
  49.8 2.3 fusion.241
  55.0 2.9 add_bitcast_fusion.1
  57.9 2.5 copy.152
  60.4 6.2 %all-to-all-start.2 = ((f32[96,128,16]{0,2,1:T(8,128)}), f32[96,128,16]{0,2,1:T(8,128)}, u32[]{:S(2)}, u32[]{:S(2)}) async-start(f32[96,128,16]{0,2,1:T(8,128)} %copy.152), calls=%async_computation.2 | async-start | bytes 2097152 | tf_op jit(solution)/shard_map/all_to_all | solution.py:101
  66.6 2.5 copy.150
  69.1 25.9 %all-to-all-done.2 = f32[96,128,16]{0,2,1:T(8,128)} async-done(((f32[96,128,16]{0,2,1:T(8,128)}), f32[96,128,16]{0,2,1:T(8,128)}, u32[]{:S(2)}, u32[]{:S(2)}) %all-to-all-start.2) | async-done | bytes 786464 | tf_op jit(solution)/shard_map/all_to_all | solution.py:101
  95.1 6.8 %all-to-all-start.1 = ((f32[96,128,16]{0,2,1:T(8,128)}), f32[96,128,16]{0,2,1:T(8,128)}, u32[]{:S(2)}, u32[]{:S(2)}) async-start(f32[96,128,16]{0,2,1:T(8,128)} %copy.150), calls=%async_computation.1 | async-start | bytes 2097152 | tf_op jit(solution)/shard_map/all_to_all | solution.py:100
  102.4 3.8 fusion.14
  106.2 23.7 %all-to-all-done.1 = f32[96,128,16]{0,2,1:T(8,128)} async-done(((f32[96,128,16]{0,2,1:T(8,128)}), f32[96,128,16]{0,2,1:T(8,128)}, u32[]{:S(2)}, u32[]{:S(2)}) %all-to-all-start.1) | async-done | bytes 786464 | tf_op jit(solution)/shard_map/all_to_all | solution.py:100
  129.9 2.9 fusion.18
  132.9 2.9 fusion.7
  135.8 3.4 subtract_bitcast_fusion
  165.0 6.4 %all-to-all-start.3 = ((f32[96,2,1024]{0,1,2:T(2,128)}), f32[96,2,1024]{0,1,2:T(2,128)}, u32[]{:S(2)}, u32[]{:S(2)}) async-start(f32[96,2,1024]{0,1,2:T(2,128)} %copy.166), calls=%async_computation.3 | async-start | bytes 2097152 | tf_op jit(solution)/shard_map/all_to_all | solution.py:147
  171.3 3.0 copy.170
  174.4 25.4 %all-to-all-done.3 = f32[96,2,1024]{0,1,2:T(2,128)} async-done(((f32[96,2,1024]{0,1,2:T(2,128)}), f32[96,2,1024]{0,1,2:T(2,128)}, u32[]{:S(2)}, u32[]{:S(2)}) %all-to-all-start.3) | async-done | bytes 786464 | tf_op jit(solution)/shard_map/all_to_all | solution.py:147
  199.8 6.4 %all-to-all-start.4 = ((f32[96,2,1024]{0,1,2:T(2,128)}), f32[96,2,1024]{0,1,2:T(2,128)}, u32[]{:S(2)}, u32[]{:S(2)}) async-start(f32[96,2,1024]{0,1,2:T(2,128)} %copy.170), calls=%async_computation.4 | async-start | bytes 2097152 | tf_op jit(solution)/shard_map/all_to_all | solution.py:148
  209.5 25.2 %all-to-all-done.4 = f32[96,2,1024]{0,1,2:T(2,128)} async-done(((f32[96,2,1024]{0,1,2:T(2,128)}), f32[96,2,1024]{0,1,2:T(2,128)}, u32[]{:S(2)}, u32[]{:S(2)}) %all-to-all-start.4) | async-done | bytes 786464 | tf_op jit(solution)/shard_map/all_to_all | solution.py:148
  242.3 6.5 %all-to-all-start.5 = ((f32[64,1,1024]{2,1,0:T(1,128)}), f32[64,1,1024]{2,1,0:T(1,128)}, u32[]{:S(2)}, u32[]{:S(2)}) async-start(f32[64,1,1024]{2,1,0:T(1,128)} %reshape.322), calls=%async_computation.5 | async-start | bytes 524288 | tf_op jit(solution)/shard_map/all_to_all | solution.py:156
  248.8 2.2 copy.175
  252.8 2.2 convolution_multiply_fusion.4
  255.1 3.0 fusion.43
  258.1 77.9 %psum.23 = f32[32,64]{1,0:T(8,128)S(1)} all-reduce(f32[32,64]{1,0:T(8,128)S(1)} %fusion.43), channel_id=1, replica_groups=mesh['seq'=64,'ch'=4] {'seq','ch'}, use_global_device_ids=true, to_apply=%region_5.6 | all-reduce | flops 2048 | bytes 16384 | tf_op jit(solution)/shard_map/psum | solution.py:182
  337.4 2.9 reduce.2
  344.0 2.8 collective-permute-start.1
  351.5 241.4 %all-reduce = (f32[3,32,3]{1,0,2:T(4,128)S(1)}, f32[64,32]{0,1:T(8,128)S(1)}) all-reduce(f32[3,32,3]{1,0,2:T(4,128)S(1)} %pad_maximum_fusion.7, f32[64,32]{0,1:T(8,128)S(1)} %fusion.238), channel_id=1, replica_groups=mesh['seq'=64,'ch'=4] {'seq'}, use_global_device_ids=true, to_apply=%region_3.4 | all-reduce | flops 2336 | bytes 18688 | tf_op jit(solution)/shard_map/psum | solution.py:181
  (110 shorter events, 65.3 us)
Async XLA Ops:
  0.6 6.9 %copy-start = (f32[32,64]{1,0:T(8,128)S(1)}, f32[32,64]{1,0:T(8,128)}, u32[]{:S(2)}) copy-start(f32[32,64]{1,0:T(8,128)} %param.9) | copy-start | bytes 24580
  0.6 12.0 %copy-start.6 = (bf16[32,1024]{1,0:T(8,128)(2,1)S(1)}, bf16[32,1024]{1,0:T(8,128)(2,1)}, u32[]{:S(2)}) copy-start(bf16[32,1024]{1,0:T(8,128)(2,1)} %param.7) | copy-start | bytes 196612
  1.5 11.3 %collective-permute-start = (bf16[3,32,2]{2,1,0:T(8,128)(2,1)S(1)}, bf16[3,32,2]{2,1,0:T(8,128)(2,1)S(1)}, u32[]{:S(2)}, u32[]{:S(2)}) collective-permute-start(bf16[3,32,2]{2,1,0:T(8,128)(2,1)S(1)} %slice.96), channel_id=1, source_target_pairs={{0,4},{4,8},{8,12},{12,16},{16,20},{20,24},{24,28},{28,32},{32,36}... | collective-permute-start | bytes 1160 | tf_op jit(solution)/shard_map/ppermute | solution.py:14
  6.5 6.3 %copy-start.10 = (s32[32]{0:T(128)}, s32[32]{0:T(128)S(1)}, u32[]{:S(2)}) copy-start(s32[32]{0:T(128)S(1)} %get-tuple-element.66) | copy-start | bytes 388
  6.5 6.3 %copy-start.12 = (pred[32]{0:T(512)(128)(4,1)}, pred[32]{0:T(512)(128)(4,1)S(1)}, u32[]{:S(2)}) copy-start(pred[32]{0:T(512)(128)(4,1)S(1)} %fusion.143) | copy-start | bytes 100
  7.5 5.3 copy-start.5
  15.1 17.7 %copy-start.9 = (f32[32]{0:T(128)S(1)}, f32[32]{0:T(128)}, u32[]{:S(2)}) copy-start(f32[32]{0:T(128)} %param.11) | copy-start | bytes 388
  15.1 17.7 %copy-start.7 = (f32[64,32]{0,1:T(8,128)S(1)}, f32[64,32]{0,1:T(8,128)}, u32[]{:S(2)}) copy-start(f32[64,32]{0,1:T(8,128)} %param.10) | copy-start | bytes 24580
  21.5 23.0 %all-to-all-start = ((f32[64,1,1024]{2,1,0:T(1,128)}), f32[64,1,1024]{2,1,0:T(1,128)}, u32[]{:S(2)}, u32[]{:S(2)}) async-start(f32[64,1,1024]{2,1,0:T(1,128)} %reshape.320), calls=%async_computation | async-start | bytes 524288 | tf_op jit(solution)/shard_map/all_to_all | solution.py:79
  52.2 1.0 copy-start.2
  60.4 34.7 %all-to-all-start.2 = ((f32[96,128,16]{0,2,1:T(8,128)}), f32[96,128,16]{0,2,1:T(8,128)}, u32[]{:S(2)}, u32[]{:S(2)}) async-start(f32[96,128,16]{0,2,1:T(8,128)} %copy.152), calls=%async_computation.2 | async-start | bytes 2097152 | tf_op jit(solution)/shard_map/all_to_all | solution.py:101
  95.1 34.9 %all-to-all-start.1 = ((f32[96,128,16]{0,2,1:T(8,128)}), f32[96,128,16]{0,2,1:T(8,128)}, u32[]{:S(2)}, u32[]{:S(2)}) async-start(f32[96,128,16]{0,2,1:T(8,128)} %copy.150), calls=%async_computation.1 | async-start | bytes 2097152 | tf_op jit(solution)/shard_map/all_to_all | solution.py:100
  129.9 3.0 copy-start.3
  165.0 34.9 %all-to-all-start.3 = ((f32[96,2,1024]{0,1,2:T(2,128)}), f32[96,2,1024]{0,1,2:T(2,128)}, u32[]{:S(2)}, u32[]{:S(2)}) async-start(f32[96,2,1024]{0,1,2:T(2,128)} %copy.166), calls=%async_computation.3 | async-start | bytes 2097152 | tf_op jit(solution)/shard_map/all_to_all | solution.py:147
  199.8 34.9 %all-to-all-start.4 = ((f32[96,2,1024]{0,1,2:T(2,128)}), f32[96,2,1024]{0,1,2:T(2,128)}, u32[]{:S(2)}, u32[]{:S(2)}) async-start(f32[96,2,1024]{0,1,2:T(2,128)} %copy.170), calls=%async_computation.4 | async-start | bytes 2097152 | tf_op jit(solution)/shard_map/all_to_all | solution.py:148
  236.0 1.0 copy-start.4
  240.2 12.6 %copy-start.8 = (f32[64,32]{0,1:T(8,128)S(1)}, f32[64,32]{0,1:T(8,128)}, u32[]{:S(2)}) copy-start(f32[64,32]{0,1:T(8,128)} %param.10) | copy-start | bytes 24580
  242.3 12.8 %copy-start.11 = (s32[32]{0:T(128)S(1)}, s32[32]{0:T(128)}, u32[]{:S(2)}) copy-start(s32[32]{0:T(128)} %copy-done.10) | copy-start | bytes 388
  242.3 12.8 %copy-start.13 = (pred[32]{0:T(512)(128)(4,1)S(1)}, pred[32]{0:T(512)(128)(4,1)}, u32[]{:S(2)}) copy-start(pred[32]{0:T(512)(128)(4,1)} %copy-done.12) | copy-start | bytes 100
  242.3 95.1 %all-to-all-start.5 = ((f32[64,1,1024]{2,1,0:T(1,128)}), f32[64,1,1024]{2,1,0:T(1,128)}, u32[]{:S(2)}, u32[]{:S(2)}) async-start(f32[64,1,1024]{2,1,0:T(1,128)} %reshape.322), calls=%async_computation.5 | async-start | bytes 524288 | tf_op jit(solution)/shard_map/all_to_all | solution.py:156
  344.0 5.1 collective-permute-start.1
  349.2 244.8 %copy-start.1 = (f32[32,64]{1,0:T(8,128)S(1)}, f32[32,64]{1,0:T(8,128)}, u32[]{:S(2)}) copy-start(f32[32,64]{1,0:T(8,128)} %param.9) | copy-start | bytes 24580
where the time goes:
time: 605 us; the launch traced here: 594 us
  blocking collectives  319 us (53%)
  waiting for transfers between devices  108 us (18%)
  matrix products  52.9 us (9%)
  starting transfers between devices  51.3 us (8%)
  local copies, waits for them, and re-layouts  42.8 us (7%)
  other arithmetic  18.9 us (3%)
    psum x1, blocking collectives, shards(): short_total, out_total = lax.psum((short_part, out_part), 'seq')  241 us
    psum x1, blocking collectives, shards(): in_total = lax.psum(in_part, ('seq', 'ch'))  77.9 us
    all_to_all x1, waiting for transfers between devices, shards(): lax.all_to_all(turned_imag, 'seq', split_axis=1, concat_axis=2, tiled=True)  25.9 us
    all_to_all x1, waiting for transfers between devices, shards(): lax.all_to_all(part_real, 'seq', split_axis=2, concat_axis=1, tiled=True)  25.4 us
    all_to_all x1, waiting for transfers between devices, shards(): lax.all_to_all(part_imag, 'seq', split_axis=2, concat_axis=1, tiled=True)  25.2 us
    all_to_all x1, waiting for transfers between devices, shards(): lax.all_to_all(turned_real, 'seq', split_axis=1, concat_axis=2, tiled=True)  23.7 us
    unnamed x38, local copies, waits for them, and re-layouts  12.3 us
  transfers between devices with their start and end apart: 8, of which 6 were waited for; matrix products, arithmetic and copies ran while one was open for 6% of the time, Pallas kernels for 0%

commit v1 on v0

v1 whole, which is shorter than its diff:
```python
import functools
import math

import jax
import jax.numpy as jnp
import ml_dtypes
import numpy as np
from jax import lax
from jax.experimental import pallas as pl
from jax.experimental.pallas import tpu as pltpu
from jax.sharding import PartitionSpec as P

MESH = pl.DeviceIdType.MESH
F32 = jnp.float32
BF16 = jnp.bfloat16
PRECISE = lax.Precision.HIGHEST
LANES = 128
ROWS = 8
TOKENS = ROWS * LANES
Z_SIZE = 8


def bf16_pair(table):
    high = table.astype(ml_dtypes.bfloat16)
    low = (table - high.astype(np.float64)).astype(ml_dtypes.bfloat16)
    return np.stack([high, low])


def make_tables(devices):
    outer = devices * ROWS
    length = outer * LANES
    half = outer // 2
    block = np.arange(devices // 2)
    within = np.arange(ROWS)
    fwd, back, twiddle = [], [], []
    for core in range(2):
        own = ((2 * block[:, None] + core) * ROWS + within[None, :]).reshape(-1)
        other = ((2 * block[:, None] + 1 - core) * ROWS + within[None, :]).reshape(-1)
        a = np.concatenate([own, other])
        k1 = core * half + np.arange(half)
        num = (a[None, :] * (4 * k1[:, None] + 1)) % (4 * outer)
        angle = num * (2.0 * np.pi / (4 * outer))
        matrix = np.concatenate([np.cos(angle), -np.sin(angle)], 0)
        fwd.append(bf16_pair(matrix))
        back.append(bf16_pair(np.ascontiguousarray(matrix.T)))
        num = (np.arange(LANES)[None, :] * (4 * k1[:, None] + 1)) % (4 * length)
        angle = num * (2.0 * np.pi / (4 * length))
        twiddle.append(np.stack([np.cos(angle), -np.sin(angle)]).astype(np.float32))
    b = np.arange(LANES)
    angle = (b[:, None] * b[None, :] % LANES) * (2.0 * np.pi / LANES)
    c, s = np.cos(angle), np.sin(angle)
    inner = np.block([[c, -s], [s, c]])
    return (
        np.stack(fwd),
        np.stack(back),
        np.stack(twiddle),
        bf16_pair(inner),
        bf16_pair(np.ascontiguousarray(inner.T)),
    )


def sin_small(x):
    y = x * x
    p = 1.0 / 6227020800.0
    p = p * y - 1.0 / 39916800.0
    p = p * y + 1.0 / 362880.0
    p = p * y - 1.0 / 5040.0
    p = p * y + 1.0 / 120.0
    p = p * y - 1.0 / 6.0
    return x + x * y * p


def minus_pi_times(x, n):
    return ((x - n * 3.140625) - n * 9.67502593994140625e-4) - n * 1.509957990978376e-7


def parity_sign(n):
    return 1.0 - 2.0 * (n - 2.0 * jnp.floor(n * 0.5))


def sin_cos(x):
    scaled = x * (1.0 / math.pi)
    n = jnp.floor(scaled + 0.5)
    sine = parity_sign(n) * sin_small(minus_pi_times(x, n))
    m = jnp.floor(scaled) + 1.0
    cosine = parity_sign(m) * sin_small(minus_pi_times(x, m - 0.5))
    return sine, cosine


def split(x):
    high = x.astype(BF16)
    return high, (x - high.astype(F32)).astype(BF16)


def dot_one(a, b):
    return lax.dot_general(a, b, (((1,), (0,)), ((), ())), preferred_element_type=F32)


def dot3(a, b):
    return dot_one(a[0], b[0]) + (dot_one(a[0], b[1]) + dot_one(a[1], b[0]))


def dot_exact(a, b, dims):
    return lax.dot_general(a, b, (dims, ((), ())), precision=PRECISE, preferred_element_type=F32)


def kernel(
    devices, y_size,
    proj, cot, sw, fin, fout, env_in, f1_hbm, f1t_hbm, tw_hbm, f2, f2t,
    gp_out, r1_out, r2_out,
    f1, f1t, tw, feat, hid, hcos, env, ext, kv, halo, sendb, abuf, spec, own, sx, xb, outb, retb,
    gm, halo_gm, r_own, r_core, r_x, r_z, r_y,
    tab_sem, halo_sem, in_send, in_recv, fwd_send, fwd_recv, x_send, x_recv, out_send, out_recv,
    hg_sem, red_send, red_recv,
):
    chips = devices // 2
    channels = cot.shape[0]
    length = devices * TOKENS
    half = devices * ROWS // 2
    blocks = channels // 8
    me = lax.axis_index("seq")
    yi = lax.axis_index("ch")
    q = lax.div(me, 2)
    core = lax.rem(me, 2)
    sib = me + 1 - 2 * core
    nxt = lax.rem(me + 1, devices)
    prv = lax.rem(me + devices - 1, devices)
    x_size = chips // Z_SIZE
    zi = lax.rem(q, Z_SIZE)
    xi = lax.div(q, Z_SIZE)

    def seq_dev(chip):
        return {"seq": 2 * chip + core}

    barrier = pltpu.get_barrier_semaphore()

    def greet(r, carry):
        pl.semaphore_signal(barrier, inc=1, device_id=seq_dev(lax.rem(q + r, chips)), device_id_type=MESH)
        return carry

    lax.fori_loop(1, chips, greet, 0)
    pl.semaphore_signal(barrier, inc=1, device_id={"seq": nxt}, device_id_type=MESH)
    pl.semaphore_signal(barrier, inc=1, device_id={"seq": prv}, device_id_type=MESH)

    def greet_y(r, carry):
        pl.semaphore_signal(barrier, inc=1, device_id={"ch": lax.rem(yi + r, y_size)}, device_id_type=MESH)
        return carry

    lax.fori_loop(1, y_size, greet_y, 0)

    tables = [
        pltpu.make_async_copy(f1_hbm.at[core], f1, tab_sem.at[0]),
        pltpu.make_async_copy(f1t_hbm.at[core], f1t, tab_sem.at[1]),
        pltpu.make_async_copy(tw_hbm.at[core], tw, tab_sem.at[2]),
    ]
    for copy in tables:
        copy.start()

    row = lax.broadcasted_iota(jnp.int32, feat.shape, 0)
    position = me * TOKENS + lax.broadcasted_iota(jnp.int32, feat.shape, 1)
    odd = row & 1
    phase = position * (1 + (row >> 1) * 499) - odd * (length // 4) + length // 2
    phase = (phase & (length - 1)) - length // 2
    feat[...] = sin_small((length // 4 - jnp.abs(phase)).astype(F32) * (2.0 * math.pi / length))
    preact = dot_exact(fin[...], feat[...], ((0,), (0,)))
    sine, cosine = sin_cos(preact)
    hid[...] = sine
    hcos[...] = cosine
    relative = (me * TOKENS + lax.broadcasted_iota(jnp.int32, env.shape, 1)).astype(F32) * (1.0 / length)
    env[...] = jnp.exp(env_in[:, 0:1] * relative) * env_in[:, 1:2]

    pl.semaphore_wait(barrier, chips - 1 + 2 + y_size - 1)

    halo_copy = pltpu.make_async_remote_copy(
        proj.at[:, :, TOKENS - LANES :], halo, halo_sem.at[0], halo_sem.at[1],
        device_id={"seq": nxt}, device_id_type=MESH,
    )
    halo_copy.start()

    def scatter_rows(slot, value, cb):
        for j in range(ROWS):
            sendb[slot, pl.ds(cb * 64 + j, 8, stride=8), :] = value[:, j * LANES : (j + 1) * LANES]

    def gather_rows(slot, cb):
        return jnp.concatenate(
            [retb[slot, pl.ds(cb * 64 + j, 8, stride=8), :] for j in range(ROWS)], 1
        )

    my_rows = pl.ds(pl.multiple_of(q * ROWS, ROWS), ROWS)

    def exchange(src, dst, lo, hi, send_sem, recv_sem):
        def one(r, carry):
            chip = lax.rem(q + r, chips)
            rows = pl.ds(pl.multiple_of(chip * ROWS, ROWS), ROWS)
            pltpu.make_async_remote_copy(
                src.at[lo:hi, rows], dst.at[lo:hi, my_rows], send_sem, recv_sem,
                device_id=seq_dev(chip), device_id_type=MESH,
            ).start()
            return carry

        lax.fori_loop(1, chips, one, 0)
        dst[lo:hi, my_rows] = src[lo:hi, my_rows]

    def wait_bytes(src, lo, hi, sem):
        part = src.at[lo:hi, pl.ds(0, (chips - 1) * ROWS)]
        pltpu.make_async_copy(part, part, sem).wait()

    modulated = dot_exact(fout[...], hid[...], ((0,), (0,)))
    filt = env[...] * modulated
    for cb in range(blocks):
        scatter_rows(0, filt[cb * 8 : cb * 8 + 8], cb)
    exchange(sendb, abuf, 0, 1, in_send.at[0], in_recv.at[0])

    halo_copy.wait()
    first = (me > 0).astype(F32)
    cot32 = cot[...].astype(F32)
    mixed = []
    for s in range(3):
        ext[s, :, LANES:] = proj[s].astype(F32)
        ext[s, :, :LANES] = halo[s].astype(F32) * first
        full = ext[s]
        total = sw[s, :, 0:1] * full[:, LANES:]
        for j in range(1, 3):
            total = total + sw[s, :, j : j + 1] * pltpu.roll(full, j, 1)[:, LANES:]
        mixed.append(total)
    kv[0] = mixed[1]
    kv[1] = mixed[2]
    gated = mixed[1] * mixed[2]
    grad_conv = cot32 * mixed[0]
    for cb in range(blocks):
        scatter_rows(1, gated[cb * 8 : cb * 8 + 8], cb)
        scatter_rows(2, grad_conv[cb * 8 : cb * 8 + 8], cb)
    exchange(sendb, abuf, 1, 3, in_send.at[1], in_recv.at[1])

    for copy in tables:
        copy.wait()

    def to_sibling(src, dst, slot):
        return pltpu.make_async_remote_copy(
            src, dst, fwd_send.at[slot], fwd_recv.at[slot], device_id={"seq": sib}, device_id_type=MESH
        )

    def forward(signals):
        a = jnp.concatenate([abuf[s] for s in signals], 1)
        u = dot3((f1[0], f1[1]), split(a))
        for at, s in enumerate(signals):
            ur = u[:half, at * LANES : (at + 1) * LANES]
            ui = u[half:, at * LANES : (at + 1) * LANES]
            v = jnp.concatenate([ur * tw[0] - ui * tw[1], ur * tw[1] + ui * tw[0]], 1)
            spec[s] = dot3(split(v), (f2[0], f2[1]))

    wait_bytes(abuf, 0, 1, in_recv.at[0])
    send_k = to_sibling(abuf.at[0:1, 0:half], abuf.at[0:1, half:], 0)
    send_k.start()
    send_k.wait()
    forward([0])
    wait_bytes(abuf, 1, 3, in_recv.at[1])
    send_gd = to_sibling(abuf.at[1:3, 0:half], abuf.at[1:3, half:], 1)
    send_gd.start()
    send_gd.wait()
    forward([1, 2])

    def parts(s):
        return spec[s, :, :LANES], spec[s, :, LANES:]

    def inverse_rows(re, im):
        z = dot3(split(jnp.concatenate([re, im], 1)), (f2t[0], f2t[1]))
        zr, zi_ = z[:, :LANES], z[:, LANES:]
        return jnp.concatenate([zr * tw[0] + zi_ * tw[1], zi_ * tw[0] - zr * tw[1]], 0)

    kr, ki = parts(0)
    gr, gi = parts(1)
    dr, di = parts(2)

    def finish(signals, rows_of):
        y = dot3((f1t[0], f1t[1]), split(jnp.concatenate(rows_of, 1)))
        for at, s in enumerate(signals):
            own[s] = y[:half, at * LANES : (at + 1) * LANES]
            sx[s] = y[half:, at * LANES : (at + 1) * LANES]

    def swap(lo, hi, slot):
        return pltpu.make_async_remote_copy(
            sx.at[lo:hi], xb.at[lo:hi], x_send.at[slot], x_recv.at[slot],
            device_id={"seq": sib}, device_id_type=MESH,
        )

    finish([0], [inverse_rows(dr * gr + di * gi, di * gr - dr * gi)])
    swap_k = swap(0, 1, 0)
    swap_k.start()
    conv_rows = inverse_rows(gr * kr - gi * ki, gr * ki + gi * kr)
    back_rows = inverse_rows(dr * kr + di * ki, di * kr - dr * ki)
    swap_k.wait()
    outb[0] = (own[0] + xb[0]) * (1.0 / length)
    exchange(outb, retb, 0, 1, out_send.at[0], out_recv.at[0])
    finish([1, 2], [conv_rows, back_rows])
    swap_c = swap(1, 3, 1)
    swap_c.start()
    swap_c.wait()
    for s in (1, 2):
        outb[s] = (own[s] + xb[s]) * (1.0 / length)
    exchange(outb, retb, 1, 3, out_send.at[1], out_recv.at[1])

    wait_bytes(retb, 0, 1, out_recv.at[0])
    weighted = env[...] * jnp.concatenate([gather_rows(0, cb) for cb in range(blocks)], 0)
    out_part = dot_exact(weighted, hid[...], ((1,), (1,)))
    grad_hidden = dot_exact(fout[...], weighted, ((1,), (0,))) * hcos[...]
    in_part = dot_exact(feat[...], grad_hidden, ((1,), (1,)))
    half_in = in_part.shape[0] // 2

    wait_bytes(retb, 1, 3, out_recv.at[1])
    conv_out = jnp.concatenate([gather_rows(1, cb) for cb in range(blocks)], 0)
    grad_gated = jnp.concatenate([gather_rows(2, cb) for cb in range(blocks)], 0)
    gm[0] = cot[...].astype(F32) * conv_out
    gm[1] = grad_gated * kv[1]
    gm[2] = grad_gated * kv[0]
    halo_back = pltpu.make_async_remote_copy(
        gm.at[:, :, 0:LANES], halo_gm, hg_sem.at[0], hg_sem.at[1],
        device_id={"seq": prv}, device_id_type=MESH,
    )
    halo_back.start()

    lane = lax.broadcasted_iota(jnp.int32, (channels, LANES - out_part.shape[1]), 1)
    short = jnp.zeros((channels, LANES - out_part.shape[1]), F32)
    for s in range(3):
        full = ext[s]
        for j in range(3):
            shifted = full[:, LANES:] if j == 0 else pltpu.roll(full, j, 1)[:, LANES:]
            total = jnp.sum(gm[s] * shifted, axis=1, keepdims=True)
            short = jnp.where(lane == s * 3 + j, total, short)
    r_own[0:channels] = jnp.concatenate([out_part, short], 1)
    r_own[channels:] = jnp.concatenate([in_part[:half_in], in_part[half_in:]], 1)

    red_core = pltpu.make_async_remote_copy(
        r_own, r_core, red_send.at[0], red_recv.at[0], device_id={"seq": sib}, device_id_type=MESH
    )
    red_core.start()

    halo_back.wait()
    last = (me < devices - 1).astype(F32)
    for s in range(3):
        full = jnp.concatenate([gm[s], halo_gm[s] * last], 1)
        total = sw[s, :, 0:1] * full[:, :TOKENS]
        for j in range(1, 3):
            total = total + sw[s, :, j : j + 1] * pltpu.roll(full, TOKENS + LANES - j, 1)[:, :TOKENS]
        gp_out[s] = total.astype(BF16)

    red_core.wait()

    def group_sum(buf, index, size, device_of, slot):
        def one(r, carry):
            pltpu.make_async_remote_copy(
                buf.at[index], buf.at[index], red_send.at[slot], red_recv.at[slot],
                device_id=device_of(lax.rem(index + r, size)), device_id_type=MESH,
            ).start()
            return carry

        lax.fori_loop(1, size, one, 0)
        rest = buf.at[pl.ds(0, size - 1)]
        pltpu.make_async_copy(rest, rest, red_recv.at[slot]).wait()
        pltpu.make_async_copy(rest, rest, red_send.at[slot]).wait()
        total = buf[0]
        for i in range(1, size):
            total = total + buf[i]
        return total

    r_x[xi] = r_own[...] + r_core[...]
    r_z[zi] = group_sum(r_x, xi, x_size, lambda i: seq_dev(i * Z_SIZE + zi), 1)
    total = group_sum(r_z, zi, Z_SIZE, lambda i: seq_dev(xi * Z_SIZE + i), 2)
    scale = 1.0 / math.sqrt(length)
    r1_out[...] = total[:channels] * scale
    r_y[yi] = total[channels:]
    r2_out[...] = group_sum(r_y, yi, y_size, lambda i: {"ch": i}, 3) * scale

    wait_bytes(sendb, 0, 1, in_send.at[0])
    wait_bytes(sendb, 1, 3, in_send.at[1])
    wait_bytes(outb, 0, 1, out_send.at[0])
    wait_bytes(outb, 1, 3, out_send.at[1])


def shards(devices, y_size, tables, proj, cotangent, short_w, filter_in, filter_out, rates):
    channels = cotangent.shape[0]
    feats, order = filter_in.shape
    length = devices * TOKENS
    chips = devices // 2
    half = devices * ROWS // 2
    outer = devices * ROWS
    spread = jnp.sqrt(jnp.expm1(-2.0 * rates) / jnp.expm1(-2.0 * rates / length))
    env_in = jnp.stack([-rates, 1.0 / spread], 1)
    r_rows = channels + feats // 2
    vmem = pl.BlockSpec(memory_space=pltpu.VMEM)
    anywhere = pl.BlockSpec(memory_space=pl.ANY)
    dma = pltpu.SemaphoreType.DMA
    grad_proj, r1, r2 = pl.pallas_call(
        functools.partial(kernel, devices, y_size),
        out_shape=(
            jax.ShapeDtypeStruct(proj.shape, BF16),
            jax.ShapeDtypeStruct((channels, LANES), F32),
            jax.ShapeDtypeStruct((feats // 2, LANES), F32),
        ),
        in_specs=[vmem] * 6 + [anywhere] * 3 + [vmem] * 2,
        out_specs=(vmem, vmem, vmem),
        scratch_shapes=[
            pltpu.VMEM((2, outer, outer), BF16),
            pltpu.VMEM((2, outer, outer), BF16),
            pltpu.VMEM((2, half, LANES), F32),
            pltpu.VMEM((feats, TOKENS), F32),
            pltpu.VMEM((order, TOKENS), F32),
            pltpu.VMEM((order, TOKENS), F32),
            pltpu.VMEM((channels, TOKENS), F32),
            pltpu.VMEM((3, channels, LANES + TOKENS), F32),
            pltpu.VMEM((2, channels, TOKENS), F32),
            pltpu.VMEM((3, channels, LANES), BF16),
            pltpu.VMEM((3, chips * ROWS, LANES), F32),
            pltpu.VMEM((3, outer, LANES), F32),
            pltpu.VMEM((3, half, 2 * LANES), F32),
            pltpu.VMEM((3, half, LANES), F32),
            pltpu.VMEM((3, half, LANES), F32),
            pltpu.VMEM((3, half, LANES), F32),
            pltpu.VMEM((3, half, LANES), F32),
            pltpu.VMEM((3, half, LANES), F32),
            pltpu.VMEM((3, channels, TOKENS), F32),
            pltpu.VMEM((3, channels, LANES), F32),
            pltpu.VMEM((r_rows, LANES), F32),
            pltpu.VMEM((r_rows, LANES), F32),
            pltpu.VMEM((chips // Z_SIZE, r_rows, LANES), F32),
            pltpu.VMEM((Z_SIZE, r_rows, LANES), F32),
            pltpu.VMEM((y_size, feats // 2, LANES), F32),
            dma((3,)), dma((2,)), dma((2,)), dma((2,)), dma((2,)), dma((2,)), dma((2,)), dma((2,)),
            dma((2,)), dma((2,)), dma((2,)), dma((4,)), dma((4,)),
        ],
        compiler_params=pltpu.CompilerParams(
            collective_id=0, has_side_effects=True, vmem_limit_bytes=40 << 20
        ),
    )(proj, cotangent, short_w, filter_in, filter_out, env_in, *tables)
    grad_out = r1[:, :order].T
    grad_short = r1[:, order : order + 9].reshape(channels, 3, 3).transpose(1, 0, 2)
    grad_in = jnp.concatenate([r2[:, :order], r2[:, order:]], 0)
    return grad_proj, grad_short, grad_out, grad_in


def solution(mesh):
    devices, y_size = mesh.shape["seq"], mesh.shape["ch"]
    tables = make_tables(devices)

    def run(*args):
        return shards(devices, y_size, [jnp.asarray(t) for t in tables], *args)

    return jax.shard_map(
        run,
        mesh=mesh,
        in_specs=(
            P(None, "ch", "seq"),
            P("ch", "seq"),
            P(None, "ch", None),
            P(),
            P(None, "ch"),
            P("ch"),
        ),
        out_specs=(P(None, "ch", "seq"), P(None, "ch", None), P(None, "ch"), P()),
        check_vma=False,
    )
```

time: 605 us -> 71.8 us (0.12); the launches traced: 594 us -> 71.3 us
  blocking collectives: 319 us -> 0 us
  waiting for transfers between devices: 108 us -> 0 us
  Pallas kernels: 0 us -> 57.6 us
  matrix products: 52.9 us -> 0 us
  starting transfers between devices: 51.3 us -> 0 us
  local copies, waits for them, and re-layouts: 42.8 us -> 11.8 us
  other arithmetic: 18.9 us -> 1.3 us
    psum x2 -> x0, blocking collectives: 319 us -> none  [the longest x1 241 us: shards(): short_total, out_total = lax.psum((short_part, out_part), 'seq')]
    all_to_all x6 -> x0, waiting for transfers between devices: 106 us -> none  [the longest x1 25.9 us: shards(): lax.all_to_all(turned_imag, 'seq', split_axis=1, concat_axis=2, tiled=True)]
    pallas_call x0 -> x1, Pallas kernels: none -> 57.6 us  [shards(): pl.pallas_call(functools.partial(kernel, devices, y_size), out_shape=(jax...]
    dot_general x25 -> x0, matrix products: 52.9 us -> none  [the longest x4 8.26 us: dft_axis(): imag_cos = jnp.einsum(form, imag_part, cosine, precision=PRECISE)]
    all_to_all x6 -> x0, starting transfers between devices: 43.6 us -> none  [the longest x1 11.3 us: shards(): lax.all_to_all(both_signals, 'seq', split_axis=2, concat_axis=1, tiled=True)]
    slice x9 -> x3, local copies, waits for them, and re-layouts: 8.97 us -> 0.23 us  [the longest x2 0.15 us: shards(): r1[:, order:order + 9].reshape(channels, 3, 3).transpose(1, 0, 2)]
    ppermute x2 -> x0, starting transfers between devices: 7.71 us -> none  [shifted(): return lax.ppermute(value, axis, pairs)]
    add x4 -> x0, local copies, waits for them, and re-layouts: 6.22 us -> none  [the longest x2 5.53 us: rotate(): imag_part * cosine + sign * real_part * sine]
  transfers between devices with their start and end apart: 8 -> 0, of which waited for: 6 -> 0; matrix products, arithmetic and copies ran while one was open for 6% -> 0% of each run, Pallas kernels for 0% -> 0%
where the time goes in v1:
time: 71.8 us; the launch traced here: 71.3 us
  Pallas kernels  57.6 us (80%)
  local copies, waits for them, and re-layouts  11.8 us (16%)
  other arithmetic  1.3 us (2%)
    pallas_call x1, Pallas kernels, shards(): pl.pallas_call(functools.partial(kernel, devices, y_size), out_shape=(jax...  57.6 us
    unnamed x19, local copies, waits for them, and re-layouts  10.9 us

profile of v1, /device:TPU:1, one launch (start us, length us, event | category | flops | bytes accessed | tf_op | source)
XLA Modules:
  0.0 71.3 jit_solution(12430795899387447067)
XLA Ops:
  0.6 0.7 negate_bitcast_fusion
  1.3 0.1 copy.27.env_in
  1.4 0.8 %copy.26.fout = f32[64,32]{1,0:T(8,128)S(1)} copy(f32[64,32]{0,1:T(8,128)} %param.15) | data formatting | bytes 16384 | tf_op args[4]
  2.2 0.8 %copy.25.sw = f32[3,32,3]{2,1,0:T(8,128)S(1)} copy(f32[3,32,3]{1,2,0:T(4,128)} %param.13) | data formatting | bytes 2304 | tf_op args[2]
  3.0 0.0 copy-start
  3.0 1.6 %copy-done = bf16[2,2,512,512]{3,2,1,0:T(8,128)(2,1)S(1)} copy-done((bf16[2,2,512,512]{3,2,1,0:T(8,128)(2,1)S(1)}, bf16[2,2,512,512]{3,2,1,0:T(8,128)(2,1)}, u32[]{:S(2)}) %copy-start) | copy-done | bytes 2097176
  4.6 0.0 copy-start.1
  4.6 1.6 %copy-done.1 = bf16[2,2,512,512]{3,2,1,0:T(8,128)(2,1)S(1)} copy-done((bf16[2,2,512,512]{3,2,1,0:T(8,128)(2,1)S(1)}, bf16[2,2,512,512]{3,2,1,0:T(8,128)(2,1)}, u32[]{:S(2)}) %copy-start.1) | copy-done | bytes 2097176
  6.2 0.0 copy-start.2
  6.2 1.0 %copy-done.2 = f32[2,2,256,128]{3,2,1,0:T(8,128)S(1)} copy-done((f32[2,2,256,128]{3,2,1,0:T(8,128)S(1)}, f32[2,2,256,128]{3,2,1,0:T(8,128)}, u32[]{:S(2)}) %copy-start.2) | copy-done | bytes 524312
  7.2 0.0 copy-start.3
  7.2 0.9 %copy-done.3 = bf16[2,256,256]{2,1,0:T(8,128)(2,1)S(1)} copy-done((bf16[2,256,256]{2,1,0:T(8,128)(2,1)S(1)}, bf16[2,256,256]{2,1,0:T(8,128)(2,1)}, u32[]{:S(2)}) %copy-start.3) | copy-done | bytes 262168
  8.2 0.0 copy-start.4
  8.2 0.9 %copy-done.4 = bf16[2,256,256]{2,1,0:T(8,128)(2,1)S(1)} copy-done((bf16[2,256,256]{2,1,0:T(8,128)(2,1)S(1)}, bf16[2,256,256]{2,1,0:T(8,128)(2,1)}, u32[]{:S(2)}) %copy-start.4) | copy-done | bytes 262168
  9.1 0.0 copy-start.5
  9.1 0.9 %copy-done.5 = bf16[3,32,1024]{2,1,0:T(8,128)(2,1)S(1)} copy-done((bf16[3,32,1024]{2,1,0:T(8,128)(2,1)S(1)}, bf16[3,32,1024]{2,1,0:T(8,128)(2,1)}, u32[]{:S(2)}) %copy-start.5) | copy-done | bytes 196632
  10.1 0.0 copy-start.6
  10.1 0.8 %copy-done.6 = bf16[32,1024]{1,0:T(8,128)(2,1)S(1)} copy-done((bf16[32,1024]{1,0:T(8,128)(2,1)S(1)}, bf16[32,1024]{1,0:T(8,128)(2,1)}, u32[]{:S(2)}) %copy-start.6) | copy-done | bytes 65560
  10.9 0.0 copy-start.7
  10.9 0.7 %copy-done.7 = f32[32,64]{1,0:T(8,128)S(1)} copy-done((f32[32,64]{1,0:T(8,128)S(1)}, f32[32,64]{1,0:T(8,128)}, u32[]{:S(2)}) %copy-start.7) | copy-done | bytes 8216
  11.6 57.6 %shard_map.138 = (bf16[3,32,1024]{2,1,0:T(8,128)(2,1)S(1)}, f32[32,128]{1,0:T(8,128)S(1)}, f32[16,128]{1,0:T(8,128)S(1)}) custom-call(bf16[3,32,1024]{2,1,0:T(8,128)(2,1)S(1)} %copy-done.5, bf16[32,1024]{1,0:T(8,128)(2,1)S(1)} %copy-done.6, f32[3,32,3]{2,1,0:T(8,128)S(1)} %copy.25.sw, f32[32,64]{1,0:T(8,128)S(1)} %copy-done.7, f32[64,32]{1,0:T(8,128)S(1)} %copy.26.fout, ...), custom_call_target="tpu_custom_call" | custom-call | tf_op jit(solution)/shard_map/pallas_call | solution.py:393
  69.2 0.1 slice.12
  69.3 0.1 copy.28
  69.4 0.6 reshape.11
  70.0 0.1 fusion
  70.0 0.6 pad_maximum_fusion
  70.7 0.7 copy.30
  (1 shorter events, 0.0 us)
Async XLA Ops:
  3.0 1.6 %copy-start = (bf16[2,2,512,512]{3,2,1,0:T(8,128)(2,1)S(1)}, bf16[2,2,512,512]{3,2,1,0:T(8,128)(2,1)}, u32[]{:S(2)}) copy-start(bf16[2,2,512,512]{3,2,1,0:T(8,128)(2,1)} %constant.18.clone.f1t_hbm) | copy-start | bytes 6291460
  4.6 1.6 %copy-start.1 = (bf16[2,2,512,512]{3,2,1,0:T(8,128)(2,1)S(1)}, bf16[2,2,512,512]{3,2,1,0:T(8,128)(2,1)}, u32[]{:S(2)}) copy-start(bf16[2,2,512,512]{3,2,1,0:T(8,128)(2,1)} %constant.17.clone.f1_hbm) | copy-start | bytes 6291460
  6.2 1.0 %copy-start.2 = (f32[2,2,256,128]{3,2,1,0:T(8,128)S(1)}, f32[2,2,256,128]{3,2,1,0:T(8,128)}, u32[]{:S(2)}) copy-start(f32[2,2,256,128]{3,2,1,0:T(8,128)} %constant.19.clone.tw_hbm) | copy-start | bytes 1572868
  7.2 0.9 %copy-start.3 = (bf16[2,256,256]{2,1,0:T(8,128)(2,1)S(1)}, bf16[2,256,256]{2,1,0:T(8,128)(2,1)}, u32[]{:S(2)}) copy-start(bf16[2,256,256]{2,1,0:T(8,128)(2,1)} %constant.21.clone.f2t) | copy-start | bytes 786436
  8.2 0.9 %copy-start.4 = (bf16[2,256,256]{2,1,0:T(8,128)(2,1)S(1)}, bf16[2,256,256]{2,1,0:T(8,128)(2,1)}, u32[]{:S(2)}) copy-start(bf16[2,256,256]{2,1,0:T(8,128)(2,1)} %constant.20.clone.f2) | copy-start | bytes 786436
  9.1 0.9 %copy-start.5 = (bf16[3,32,1024]{2,1,0:T(8,128)(2,1)S(1)}, bf16[3,32,1024]{2,1,0:T(8,128)(2,1)}, u32[]{:S(2)}) copy-start(bf16[3,32,1024]{2,1,0:T(8,128)(2,1)} %proj.1) | copy-start | bytes 589828
  10.1 0.8 %copy-start.6 = (bf16[32,1024]{1,0:T(8,128)(2,1)S(1)}, bf16[32,1024]{1,0:T(8,128)(2,1)}, u32[]{:S(2)}) copy-start(bf16[32,1024]{1,0:T(8,128)(2,1)} %cot.1) | copy-start | bytes 196612
  10.9 0.7 %copy-start.7 = (f32[32,64]{1,0:T(8,128)S(1)}, f32[32,64]{1,0:T(8,128)}, u32[]{:S(2)}) copy-start(f32[32,64]{1,0:T(8,128)} %fin.1) | copy-start | bytes 24580

commit v2 on v1

--- a/solution.py
+++ b/solution.py
@@ -87,6 +87,26 @@
     return sine, cosine
 
 
+def diagonal(n):
+    return lax.broadcasted_iota(jnp.int32, (n, n), 0) == lax.broadcasted_iota(jnp.int32, (n, n), 1)
+
+
+def column(row):
+    return jnp.sum(jnp.where(diagonal(row.shape[1]), row, 0.0), axis=1, keepdims=True)
+
+
+def as_row(col):
+    return jnp.sum(jnp.where(diagonal(col.shape[0]), col, 0.0), axis=0, keepdims=True)
+
+
+def inverse_spread(rate, length):
+    y = rate * (2.0 / length)
+    p = 1.0 / 5040.0
+    for k in (720.0, 120.0, 24.0, 6.0, 2.0, 1.0):
+        p = 1.0 / k - y * p
+    return jnp.sqrt(y * p / (1.0 - jnp.exp(-2.0 * rate)))
+
+
 def split(x):
     high = x.astype(BF16)
     return high, (x - high.astype(F32)).astype(BF16)
@@ -106,9 +126,9 @@
 
 def kernel(
     devices, y_size,
-    proj, cot, sw, fin, fout, env_in, f1_hbm, f1t_hbm, tw_hbm, f2, f2t,
-    gp_out, r1_out, r2_out,
-    f1, f1t, tw, feat, hid, hcos, env, ext, kv, halo, sendb, abuf, spec, own, sx, xb, outb, retb,
+    proj_hbm, cot_hbm, sw_hbm, fin_hbm, fout_hbm, rates_hbm, f1_hbm, f1t_hbm, tw_hbm, f2_hbm, f2t_hbm,
+    gp_out, short_out, fout_out, fin_out,
+    proj, cot, sw, fin, fout, rates, f1, f1t, tw, f2, f2t, feat, hid, hcos, env, ext, kv, halo, sendb, abuf, spec, own, sx, xb, outb, retb,
     gm, halo_gm, r_own, r_core, r_x, r_z, r_y,
     tab_sem, halo_sem, in_send, in_recv, fwd_send, fwd_recv, x_send, x_recv, out_send, out_recv,
     hg_sem, red_send, red_recv,
@@ -132,6 +152,13 @@
     def seq_dev(chip):
         return {"seq": 2 * chip + core}
 
+    moves = (
+        (fin_hbm, fin), (rates_hbm, rates), (fout_hbm, fout), (sw_hbm, sw), (proj_hbm, proj), (cot_hbm, cot),
+        (f1_hbm.at[core], f1), (tw_hbm.at[core], tw), (f2_hbm, f2), (f2t_hbm, f2t), (f1t_hbm.at[core], f1t),
+    )
+    loads = [pltpu.make_async_copy(src, dst, tab_sem.at[i]) for i, (src, dst) in enumerate(moves)]
+    for copy in loads:
+        copy.start()
     barrier = pltpu.get_barrier_semaphore()
 
     def greet(r, carry):
@@ -148,13 +175,6 @@
 
     lax.fori_loop(1, y_size, greet_y, 0)
 
-    tables = [
-        pltpu.make_async_copy(f1_hbm.at[core], f1, tab_sem.at[0]),
-        pltpu.make_async_copy(f1t_hbm.at[core], f1t, tab_sem.at[1]),
-        pltpu.make_async_copy(tw_hbm.at[core], tw, tab_sem.at[2]),
-    ]
-    for copy in tables:
-        copy.start()
 
     row = lax.broadcasted_iota(jnp.int32, feat.shape, 0)
     position = me * TOKENS + lax.broadcasted_iota(jnp.int32, feat.shape, 1)
@@ -162,17 +182,20 @@
     phase = position * (1 + (row >> 1) * 499) - odd * (length // 4) + length // 2
     phase = (phase & (length - 1)) - length // 2
     feat[...] = sin_small((length // 4 - jnp.abs(phase)).astype(F32) * (2.0 * math.pi / length))
+    for copy in loads[:4]:
+        copy.wait()
     preact = dot_exact(fin[...], feat[...], ((0,), (0,)))
     sine, cosine = sin_cos(preact)
     hid[...] = sine
     hcos[...] = cosine
     relative = (me * TOKENS + lax.broadcasted_iota(jnp.int32, env.shape, 1)).astype(F32) * (1.0 / length)
-    env[...] = jnp.exp(env_in[:, 0:1] * relative) * env_in[:, 1:2]
+    rate = column(rates[...])
+    env[...] = jnp.exp(-rate * relative) * inverse_spread(rate, length)
 
     pl.semaphore_wait(barrier, chips - 1 + 2 + y_size - 1)
 
     halo_copy = pltpu.make_async_remote_copy(
-        proj.at[:, :, TOKENS - LANES :], halo, halo_sem.at[0], halo_sem.at[1],
+        proj_hbm.at[:, :, TOKENS - LANES :], halo, halo_sem.at[0], halo_sem.at[1],
         device_id={"seq": nxt}, device_id_type=MESH,
     )
     halo_copy.start()
@@ -205,12 +228,15 @@
         part = src.at[lo:hi, pl.ds(0, (chips - 1) * ROWS)]
         pltpu.make_async_copy(part, part, sem).wait()
 
-    modulated = dot_exact(fout[...], hid[...], ((0,), (0,)))
+    modulated = dot_exact(fout[...], hid[...], ((1,), (0,)))
     filt = env[...] * modulated
     for cb in range(blocks):
         scatter_rows(0, filt[cb * 8 : cb * 8 + 8], cb)
     exchange(sendb, abuf, 0, 1, in_send.at[0], in_recv.at[0])
 
+    for copy in loads[4:6]:
+        copy.wait()
+    taps = [[column(sw[s, j : j + 1, :]) for j in range(3)] for s in range(3)]
     halo_copy.wait()
     first = (me > 0).astype(F32)
     cot32 = cot[...].astype(F32)
@@ -219,9 +245,9 @@
         ext[s, :, LANES:] = proj[s].astype(F32)
         ext[s, :, :LANES] = halo[s].astype(F32) * first
         full = ext[s]
-        total = sw[s, :, 0:1] * full[:, LANES:]
+        total = taps[s][0] * full[:, LANES:]
         for j in range(1, 3):
-            total = total + sw[s, :, j : j + 1] * pltpu.roll(full, j, 1)[:, LANES:]
+            total = total + taps[s][j] * pltpu.roll(full, j, 1)[:, LANES:]
         mixed.append(total)
     kv[0] = mixed[1]
     kv[1] = mixed[2]
@@ -232,7 +258,7 @@
         scatter_rows(2, grad_conv[cb * 8 : cb * 8 + 8], cb)
     exchange(sendb, abuf, 1, 3, in_send.at[1], in_recv.at[1])
 
-    for copy in tables:
+    for copy in loads[6:]:
         copy.wait()
 
     def to_sibling(src, dst, slot):
@@ -303,7 +329,7 @@
     wait_bytes(retb, 0, 1, out_recv.at[0])
     weighted = env[...] * jnp.concatenate([gather_rows(0, cb) for cb in range(blocks)], 0)
     out_part = dot_exact(weighted, hid[...], ((1,), (1,)))
-    grad_hidden = dot_exact(fout[...], weighted, ((1,), (0,))) * hcos[...]
+    grad_hidden = dot_exact(fout[...], weighted, ((0,), (0,))) * hcos[...]
     in_part = dot_exact(feat[...], grad_hidden, ((1,), (1,)))
     half_in = in_part.shape[0] // 2
 
@@ -339,9 +365,9 @@
     last = (me < devices - 1).astype(F32)
     for s in range(3):
         full = jnp.concatenate([gm[s], halo_gm[s] * last], 1)
-        total = sw[s, :, 0:1] * full[:, :TOKENS]
+        total = taps[s][0] * full[:, :TOKENS]
         for j in range(1, 3):
-            total = total + sw[s, :, j : j + 1] * pltpu.roll(full, TOKENS + LANES - j, 1)[:, :TOKENS]
+            total = total + taps[s][j] * pltpu.roll(full, TOKENS + LANES - j, 1)[:, :TOKENS]
         gp_out[s] = total.astype(BF16)
 
     red_core.wait()
@@ -367,9 +393,16 @@
     r_z[zi] = group_sum(r_x, xi, x_size, lambda i: seq_dev(i * Z_SIZE + zi), 1)
     total = group_sum(r_z, zi, Z_SIZE, lambda i: seq_dev(xi * Z_SIZE + i), 2)
     scale = 1.0 / math.sqrt(length)
-    r1_out[...] = total[:channels] * scale
+    units = hid.shape[0]
+    fout_out[...] = total[:channels, :units] * scale
+    for s in range(3):
+        short_out[s] = jnp.concatenate(
+            [as_row(total[:channels, units + 3 * s + j : units + 3 * s + j + 1]) for j in range(3)], 0
+        ) * scale
     r_y[yi] = total[channels:]
-    r2_out[...] = group_sum(r_y, yi, y_size, lambda i: {"ch": i}, 3) * scale
+    in_total = group_sum(r_y, yi, y_size, lambda i: {"ch": i}, 3) * scale
+    fin_out[0:half_in] = in_total[:, :units]
+    fin_out[half_in:] = in_total[:, units:]
 
     wait_bytes(sendb, 0, 1, in_send.at[0])
     wait_bytes(sendb, 1, 3, in_send.at[1])
@@ -384,25 +417,32 @@
     chips = devices // 2
     half = devices * ROWS // 2
     outer = devices * ROWS
-    spread = jnp.sqrt(jnp.expm1(-2.0 * rates) / jnp.expm1(-2.0 * rates / length))
-    env_in = jnp.stack([-rates, 1.0 / spread], 1)
     r_rows = channels + feats // 2
     vmem = pl.BlockSpec(memory_space=pltpu.VMEM)
-    anywhere = pl.BlockSpec(memory_space=pl.ANY)
+    hbm = pl.BlockSpec(memory_space=pltpu.HBM)
     dma = pltpu.SemaphoreType.DMA
-    grad_proj, r1, r2 = pl.pallas_call(
+    grad_proj, grad_short, grad_out, grad_in = pl.pallas_call(
         functools.partial(kernel, devices, y_size),
         out_shape=(
             jax.ShapeDtypeStruct(proj.shape, BF16),
-            jax.ShapeDtypeStruct((channels, LANES), F32),
-            jax.ShapeDtypeStruct((feats // 2, LANES), F32),
+            jax.ShapeDtypeStruct((3, 3, channels), F32),
+            jax.ShapeDtypeStruct((channels, order), F32),
+            jax.ShapeDtypeStruct((feats, order), F32),
         ),
-        in_specs=[vmem] * 6 + [anywhere] * 3 + [vmem] * 2,
-        out_specs=(vmem, vmem, vmem),
+        in_specs=[hbm] * 11,
+        out_specs=(vmem,) * 4,
         scratch_shapes=[
+            pltpu.VMEM(proj.shape, BF16),
+            pltpu.VMEM(cotangent.shape, BF16),
+            pltpu.VMEM((3, 3, channels), F32),
+            pltpu.VMEM((feats, order), F32),
+            pltpu.VMEM((channels, order), F32),
+            pltpu.VMEM((1, channels), F32),
             pltpu.VMEM((2, outer, outer), BF16),
             pltpu.VMEM((2, outer, outer), BF16),
             pltpu.VMEM((2, half, LANES), F32),
+            pltpu.VMEM((2, 2 * LANES, 2 * LANES), BF16),
+            pltpu.VMEM((2, 2 * LANES, 2 * LANES), BF16),
             pltpu.VMEM((feats, TOKENS), F32),
             pltpu.VMEM((order, TOKENS), F32),
             pltpu.VMEM((order, TOKENS), F32),
@@ -425,17 +465,14 @@
             pltpu.VMEM((chips // Z_SIZE, r_rows, LANES), F32),
             pltpu.VMEM((Z_SIZE, r_rows, LANES), F32),
             pltpu.VMEM((y_size, feats // 2, LANES), F32),
-            dma((3,)), dma((2,)), dma((2,)), dma((2,)), dma((2,)), dma((2,)), dma((2,)), dma((2,)),
+            dma((11,)), dma((2,)), dma((2,)), dma((2,)), dma((2,)), dma((2,)), dma((2,)), dma((2,)),
             dma((2,)), dma((2,)), dma((2,)), dma((4,)), dma((4,)),
         ],
         compiler_params=pltpu.CompilerParams(
-            collective_id=0, has_side_effects=True, vmem_limit_bytes=40 << 20
+            collective_id=0, has_side_effects=True, vmem_limit_bytes=56 << 20
         ),
-    )(proj, cotangent, short_w, filter_in, filter_out, env_in, *tables)
-    grad_out = r1[:, :order].T
-    grad_short = r1[:, order : order + 9].reshape(channels, 3, 3).transpose(1, 0, 2)
-    grad_in = jnp.concatenate([r2[:, :order], r2[:, order:]], 0)
-    return grad_proj, grad_short, grad_out, grad_in
+    )(proj, cotangent, short_w.transpose(0, 2, 1), filter_in, filter_out.T, rates.reshape(1, channels), *tables)
+    return grad_proj, grad_short.transpose(0, 2, 1), grad_out.T, grad_in
 
 
 def solution(mesh):

time: 71.8 us -> 65.3 us (0.909)
  local copies, waits for them, and re-layouts: 11.8 us -> 5.55 us
  other arithmetic: 1.3 us -> 0 us
  Pallas kernels: 57.6 us -> 58.7 us
    unnamed x19 -> x4, local copies, waits for them, and re-layouts: 10.9 us -> 5.55 us
    pallas_call x1, Pallas kernels: 57.6 us -> 58.7 us  [shards(): pl.pallas_call(functools.partial(kernel, devices, y_size), out_shape=(jax...]
where the time goes in v2:
time: 65.3 us; the launch traced here: 64.9 us
  Pallas kernels  58.7 us (90%)
  local copies, waits for them, and re-layouts  5.55 us (8%)
    pallas_call x1, Pallas kernels, shards(): pl.pallas_call(functools.partial(kernel, devices, y_size), out_shape=(jax...  58.7 us
    unnamed x4, local copies, waits for them, and re-layouts  5.55 us

profile of v2, /device:TPU:1, one launch (start us, length us, event | category | flops | bytes accessed | tf_op | source)
XLA Modules:
  0.0 64.9 jit_solution(10899441219178980776)
XLA Ops:
  0.6 58.7 %shard_map.138 = (bf16[3,32,1024]{2,1,0:T(8,128)(2,1)}, f32[3,3,32]{2,1,0:T(4,128)}, f32[32,64]{1,0:T(8,128)}, f32[32,64]{1,0:T(8,128)}) custom-call(bf16[3,32,1024]{2,1,0:T(8,128)(2,1)} %proj_hbm.1, bf16[32,1024]{1,0:T(8,128)(2,1)} %cot_hbm.1, f32[3,3,32]{2,1,0:T(4,128)} %bitcast.7, f32[32,64]{1,0:T(8,128)} %fin_hbm.1, f32[32,64]{1,0:T(8,128)} %bitcast.5, ...), custom_call_target="tpu_custom_call" | custom-call | tf_op jit(solution)/shard_map/pallas_call | solution.py:424
  59.3 1.6 %copy.19 = bf16[3,32,1024]{2,1,0:T(8,128)(2,1)} copy(bf16[3,32,1024]{2,1,0:T(8,128)(2,1)} %get-tuple-element.16) | data formatting | bytes 393216
  61.0 1.3 %copy.20 = f32[3,32,3]{1,2,0:T(4,128)} copy(f32[3,32,3]{1,2,0:T(4,128)} %bitcast.8) | data formatting | bytes 2304
  62.2 1.3 %copy.21 = f32[64,32]{0,1:T(8,128)} copy(f32[64,32]{0,1:T(8,128)} %bitcast.6) | data formatting | bytes 16384
  63.6 1.3 %copy.22 = f32[32,64]{1,0:T(8,128)} copy(f32[32,64]{1,0:T(8,128)} %get-tuple-element.19) | data formatting | bytes 16384

commit v3 on v2

v3 whole, which is shorter than its diff:
```python
import functools
import math

import jax
import jax.numpy as jnp
import ml_dtypes
import numpy as np
from jax import lax
from jax.experimental import pallas as pl
from jax.experimental.pallas import tpu as pltpu
from jax.sharding import PartitionSpec as P

MESH = pl.DeviceIdType.MESH
F32 = jnp.float32
BF16 = jnp.bfloat16
PRECISE = lax.Precision.HIGHEST
LANES = 128
ROWS = 8
TOKENS = ROWS * LANES


def bf16_pair(table):
    high = table.astype(ml_dtypes.bfloat16)
    low = (table - high.astype(np.float64)).astype(ml_dtypes.bfloat16)
    return np.stack([high, low])


def make_tables(devices):
    outer = devices * ROWS
    length = outer * LANES
    half = outer // 2
    a = np.arange(outer)
    fwd, back, twiddle = [], [], []
    for core in range(2):
        k1 = core * half + np.arange(half)
        num = (a[None, :] * (4 * k1[:, None] + 1)) % (4 * outer)
        angle = num * (2.0 * np.pi / (4 * outer))
        matrix = np.concatenate([np.cos(angle), -np.sin(angle)], 0)
        fwd.append(bf16_pair(matrix))
        back.append(bf16_pair(np.ascontiguousarray(matrix.T)))
        num = (np.arange(LANES)[None, :] * (4 * k1[:, None] + 1)) % (4 * length)
        angle = num * (2.0 * np.pi / (4 * length))
        twiddle.append(np.stack([np.cos(angle), -np.sin(angle)]).astype(np.float32))
    b = np.arange(LANES)
    angle = (b[:, None] * b[None, :] % LANES) * (2.0 * np.pi / LANES)
    c, s = np.cos(angle), np.sin(angle)
    inner = np.block([[c, -s], [s, c]])
    return (
        np.stack(fwd),
        np.stack(back),
        np.stack(twiddle),
        bf16_pair(inner),
        bf16_pair(np.ascontiguousarray(inner.T)),
    )


def sin_small(x):
    y = x * x
    p = 1.0 / 6227020800.0
    p = p * y - 1.0 / 39916800.0
    p = p * y + 1.0 / 362880.0
    p = p * y - 1.0 / 5040.0
    p = p * y + 1.0 / 120.0
    p = p * y - 1.0 / 6.0
    return x + x * y * p


def minus_pi_times(x, n):
    return ((x - n * 3.140625) - n * 9.67502593994140625e-4) - n * 1.509957990978376e-7


def parity_sign(n):
    return 1.0 - 2.0 * (n - 2.0 * jnp.floor(n * 0.5))


def sin_cos(x):
    scaled = x * (1.0 / math.pi)
    n = jnp.floor(scaled + 0.5)
    sine = parity_sign(n) * sin_small(minus_pi_times(x, n))
    m = jnp.floor(scaled) + 1.0
    cosine = parity_sign(m) * sin_small(minus_pi_times(x, m - 0.5))
    return sine, cosine


def diagonal(n):
    return lax.broadcasted_iota(jnp.int32, (n, n), 0) == lax.broadcasted_iota(jnp.int32, (n, n), 1)


def column(row):
    return jnp.sum(jnp.where(diagonal(row.shape[1]), row, 0.0), axis=1, keepdims=True)


def as_row(col):
    return jnp.sum(jnp.where(diagonal(col.shape[0]), col, 0.0), axis=0, keepdims=True)


def inverse_spread(rate, length):
    y = rate * (2.0 / length)
    p = 1.0 / 5040.0
    for k in (720.0, 120.0, 24.0, 6.0, 2.0, 1.0):
        p = 1.0 / k - y * p
    return jnp.sqrt(y * p / (1.0 - jnp.exp(-2.0 * rate)))


def split(x):
    high = x.astype(BF16)
    return high, (x - high.astype(F32)).astype(BF16)


def dot_one(a, b):
    return lax.dot_general(a, b, (((1,), (0,)), ((), ())), preferred_element_type=F32)


def dot3(a, b):
    return dot_one(a[0], b[0]) + (dot_one(a[0], b[1]) + dot_one(a[1], b[0]))


def dot_exact(a, b, dims):
    return lax.dot_general(a, b, (dims, ((), ())), precision=PRECISE, preferred_element_type=F32)


def kernel(
    devices, y_size,
    proj_hbm, cot_hbm, sw_hbm, fin_hbm, fout_hbm, rates_hbm, f1_hbm, f1t_hbm, tw_hbm, f2_hbm, f2t_hbm,
    gp_out, short_out, fout_out, fin_out,
    proj, cot, sw, fin, fout, rates, f1, f1t, tw, f2, f2t,
    feat, hid, hcos, env, raw32, raw_send, raw, k_send, kbuf, shifts, kv, spec, ybuf, xb, kg_send, kg_ret,
    res, gp_send, gp_ret, gp32, gp, row_send, row_in, row_mid, row_all, s_own, s_sib, s_all, small, short_rows,
    load_sem, in_send, in_recv, sib_send, sib_recv, x_send, x_recv, ret_send, ret_recv,
    red_send, red_recv, store_sem,
):
    chips = devices // 2
    channels = cot.shape[0]
    length = devices * TOKENS
    outer = devices * ROWS
    half = outer // 2
    local = half + ROWS
    blocks = channels // 8
    units = hid.shape[0]
    me = lax.axis_index("seq")
    yi = lax.axis_index("ch")
    q = lax.div(me, 2)
    core = lax.rem(me, 2)
    sib = me + 1 - 2 * core

    def seq_dev(chip):
        return {"seq": 2 * chip + core}

    barrier = pltpu.get_barrier_semaphore()

    def greet(r, carry):
        pl.semaphore_signal(barrier, inc=1, device_id={"seq": lax.rem(me + r, devices)}, device_id_type=MESH)
        return carry

    lax.fori_loop(1, devices, greet, 0)

    def cross(r):
        y = lax.rem(yi + lax.div(r, 2), y_size)
        return {"ch": y, "seq": 2 * q + lax.rem(core + r, 2)}

    def greet_y(r, carry):
        pl.semaphore_signal(barrier, inc=1, device_id=cross(r), device_id_type=MESH)
        return carry

    lax.fori_loop(2, 2 * y_size, greet_y, 0)

    moves = (
        (fin_hbm, fin), (rates_hbm, rates), (fout_hbm, fout), (proj_hbm, proj), (cot_hbm, cot), (sw_hbm, sw),
        (f1_hbm.at[core], f1), (tw_hbm.at[core], tw), (f2_hbm, f2), (f2t_hbm, f2t), (f1t_hbm.at[core], f1t),
    )
    loads = [pltpu.make_async_copy(src, dst, load_sem.at[i]) for i, (src, dst) in enumerate(moves)]
    for copy in loads:
        copy.start()

    def remote(src, dst, send_sem, recv_sem, device):
        return pltpu.make_async_remote_copy(
            src, dst, send_sem, recv_sem, device_id=device, device_id_type=MESH
        )

    def wait_bytes(part, sem):
        pltpu.make_async_copy(part, part, sem).wait()

    row = lax.broadcasted_iota(jnp.int32, feat.shape, 0)
    position = me * TOKENS + lax.broadcasted_iota(jnp.int32, feat.shape, 1)
    odd = row & 1
    phase = position * (1 + (row >> 1) * 499) - odd * (length // 4) + length // 2
    phase = (phase & (length - 1)) - length // 2
    feat[...] = sin_small((length // 4 - jnp.abs(phase)).astype(F32) * (2.0 * math.pi / length))
    for copy in loads[:5]:
        copy.wait()

    for s in range(4):
        value = cot[...].astype(F32) if s == 3 else proj[s].astype(F32)
        for cb in range(blocks):
            for j in range(ROWS):
                rows = pl.ds(cb * 8 * 4 * ROWS + s * ROWS + j, 8, stride=4 * ROWS)
                raw32[rows, :] = value[cb * 8 : cb * 8 + 8, j * LANES : (j + 1) * LANES]
    raw_send[...] = raw32[...].reshape(raw_send.shape).astype(BF16)

    preact = dot_exact(fin[...], feat[...], ((0,), (0,)))
    sine, cosine = sin_cos(preact)
    hid[...] = sine
    hcos[...] = cosine
    relative = (me * TOKENS + lax.broadcasted_iota(jnp.int32, env.shape, 1)).astype(F32) * (1.0 / length)
    rate = column(rates[...])
    env[...] = jnp.exp(-rate * relative) * inverse_spread(rate, length)
    filt = env[...] * dot_exact(fout[...], hid[...], ((1,), (0,)))
    for cb in range(blocks):
        for j in range(ROWS):
            k_send[pl.ds(cb * 64 + j, 8, stride=8), :] = filt[cb * 8 : cb * 8 + 8, j * LANES : (j + 1) * LANES]

    pl.semaphore_wait(barrier, devices - 1 + 2 * y_size - 2)

    def rows_of(chip):
        return pl.ds(pl.multiple_of(chip * ROWS, ROWS), ROWS)

    def to_chips(start):
        def one(r, carry):
            start(lax.rem(q + r, chips))
            return carry

        lax.fori_loop(1, chips, one, 0)

    to_chips(
        lambda chip: remote(
            raw_send.at[chip], raw.at[q, core], in_send.at[0], in_recv.at[0], seq_dev(chip)
        ).start()
    )
    raw[q, core] = raw_send[q]
    to_chips(
        lambda chip: remote(
            k_send.at[rows_of(chip)], kbuf.at[q, core], in_send.at[1], in_recv.at[1], seq_dev(chip)
        ).start()
    )
    kbuf[q, core] = k_send[rows_of(q)]

    for copy in loads[5:]:
        copy.wait()
    lane9 = lax.broadcasted_iota(jnp.int32, (1, channels), 1)
    taps = [
        [jnp.sum(jnp.where(lane9 == q, sw[s, j : j + 1, :], 0.0), axis=1, keepdims=True) for j in range(3)]
        for s in range(3)
    ]

    wait_bytes(raw_send.at[pl.ds(0, chips - 1)], in_recv.at[0])
    sib_raw = remote(raw.at[:, core], raw.at[:, core], sib_send.at[0], sib_recv.at[0], {"seq": sib})
    sib_raw.start()
    sib_raw.wait()

    lane = lax.broadcasted_iota(jnp.int32, (outer, LANES), 1)
    line = lax.broadcasted_iota(jnp.int32, (outer, LANES), 0)
    mixed = []
    for s in range(3):
        x = raw[:, :, s].astype(F32).reshape(outer, LANES)
        total = taps[s][0] * x
        for j in range(1, 3):
            turned = pltpu.roll(x, j, 1)
            before = jnp.where(line == 0, 0.0, pltpu.roll(turned, 1, 0))
            moved = jnp.where(lane < j, before, turned)
            shifts[s, j - 1] = moved
            total = total + taps[s][j] * moved
        mixed.append(total)
    kv[0] = mixed[1]
    kv[1] = mixed[2]
    gated = mixed[1] * mixed[2]
    grad_conv = raw[:, :, 3].astype(F32).reshape(outer, LANES) * mixed[0]

    def forward(values, slots):
        u = dot3((f1[0], f1[1]), split(jnp.concatenate(values, 1) if len(values) > 1 else values[0]))
        for at, s in enumerate(slots):
            ur = u[:half, at * LANES : (at + 1) * LANES]
            ui = u[half:, at * LANES : (at + 1) * LANES]
            v = jnp.concatenate([ur * tw[0] - ui * tw[1], ur * tw[1] + ui * tw[0]], 1)
            spec[s] = dot3(split(v), (f2[0], f2[1]))

    def parts(s):
        return spec[s, :, :LANES], spec[s, :, LANES:]

    def inverse_rows(re, im):
        z = dot3(split(jnp.concatenate([re, im], 1)), (f2t[0], f2t[1]))
        zr, zi = z[:, :LANES], z[:, LANES:]
        return jnp.concatenate([zr * tw[0] + zi * tw[1], zi * tw[0] - zr * tw[1]], 0)

    def finish(slots, columns):
        y = dot3((f1t[0], f1t[1]), split(jnp.concatenate(columns, 1) if len(columns) > 1 else columns[0]))
        for at, s in enumerate(slots):
            ybuf[s] = y[:, at * LANES : (at + 1) * LANES]

    mine = pl.ds(pl.multiple_of(core * (half - ROWS), ROWS), local)
    theirs = pl.ds(pl.multiple_of((1 - core) * (half - ROWS), ROWS), local)

    def swap(lo, hi, slot):
        return remote(
            ybuf.at[lo:hi, theirs], xb.at[lo:hi], x_send.at[slot], x_recv.at[slot], {"seq": sib}
        )

    forward([gated, grad_conv], [1, 2])
    gr, gi = parts(1)
    dr, di = parts(2)
    finish([0], [inverse_rows(dr * gr + di * gi, di * gr - dr * gi)])
    swap_k = swap(0, 1, 0)
    swap_k.start()

    wait_bytes(k_send.at[pl.ds(0, (chips - 1) * ROWS)], in_recv.at[1])
    sib_k = remote(kbuf.at[:, core], kbuf.at[:, core], sib_send.at[1], sib_recv.at[1], {"seq": sib})
    sib_k.start()

    def send_half(src, dst, slot):
        def one(r, carry):
            d = lax.rem(q + r, chips)
            target = core * chips + d

            @pl.when(target != me)
            def _():
                remote(src.at[d], dst.at[q], ret_send.at[slot], ret_recv.at[slot], {"seq": target}).start()

            @pl.when(target == me)
            def _():
                pltpu.make_async_copy(src.at[d], dst.at[q], ret_recv.at[slot]).start()

            return carry

        lax.fori_loop(0, chips, one, 0)

    swap_k.wait()
    own_rows = pl.ds(pl.multiple_of(core * ROWS, ROWS), half)
    kg = (ybuf[0, pl.ds(pl.multiple_of(core * half, ROWS), half), :] + xb[0, own_rows, :]) * (1.0 / length)
    kg_send[...] = kg.reshape(kg_send.shape)
    send_half(kg_send, kg_ret, 0)

    sib_k.wait()
    forward([kbuf[...].reshape(outer, LANES)], [0])
    kr, ki = parts(0)
    finish(
        [1, 2],
        [
            inverse_rows(gr * kr - gi * ki, gr * ki + gi * kr),
            inverse_rows(dr * kr + di * ki, di * kr - dr * ki),
        ],
    )
    swap_c = swap(1, 3, 1)
    swap_c.start()
    swap_c.wait()

    conv_out = (ybuf[1, mine, :] + xb[1]) * (1.0 / length)
    grad_gated = (ybuf[2, mine, :] + xb[2]) * (1.0 / length)
    lane = lax.broadcasted_iota(jnp.int32, (local, LANES), 1)
    line = lax.broadcasted_iota(jnp.int32, (local, LANES), 0)
    is_mine = (line >= core * ROWS) & (line < core * ROWS + half)
    cot_all = raw[:, :, 3].astype(F32).reshape(outer, LANES)
    gp32[0:outer, :] = cot_all
    cot_mine = gp32[mine, :]
    grad_mixed = [cot_mine * conv_out, grad_gated * kv[1, mine, :], grad_gated * kv[0, mine, :]]
    for s in range(3):
        g = grad_mixed[s]
        total = taps[s][0] * g
        for j in range(1, 3):
            turned = pltpu.roll(g, LANES - j, 1)
            after = jnp.where(line == local - 1, 0.0, pltpu.roll(turned, local - 1, 0))
            total = total + taps[s][j] * jnp.where(lane >= LANES - j, after, turned)
        res[s] = total
        gp_send[:, s] = res[s, own_rows, :].reshape(chips, ROWS, LANES).astype(BF16)
    send_half(gp_send, gp_ret, 1)

    lane1 = lax.broadcasted_iota(jnp.int32, (1, LANES), 1)
    short = jnp.zeros((1, LANES), F32)
    for s in range(3):
        g = jnp.where(is_mine, grad_mixed[s], 0.0)
        gp32[0:outer, :] = raw[:, :, s].astype(F32).reshape(outer, LANES)
        for j in range(3):
            x = gp32[mine, :] if j == 0 else shifts[s, j - 1, mine, :]
            total = jnp.sum(jnp.sum(g * x, axis=0, keepdims=True), axis=1, keepdims=True)
            short = jnp.where(lane1 == s * 3 + j, total, short)
    s_own[...] = short
    sib_short = remote(s_own, s_sib, sib_send.at[2], sib_recv.at[2], {"seq": sib})
    sib_short.start()

    wait_bytes(kg_send, ret_recv.at[0])
    weighted = env[...] * jnp.concatenate(
        [
            jnp.concatenate(
                [
                    kg_ret.at[pl.ds(cb * 8, 8)][:, j, :] for j in range(ROWS)
                ], 1,
            )
            for cb in range(blocks)
        ], 0,
    )
    out_part = dot_exact(weighted, hid[...], ((1,), (1,)))
    grad_hidden = dot_exact(fout[...], weighted, ((0,), (0,))) * hcos[...]
    in_part = dot_exact(feat[...], grad_hidden, ((1,), (1,)))
    row_send[...] = jnp.concatenate([out_part, in_part], 1).reshape(row_send.shape)
    to_chips(
        lambda chip: remote(
            row_send.at[chip], row_in.at[q], red_send.at[0], red_recv.at[0], seq_dev(chip)
        ).start()
    )
    row_in[q] = row_send[q]

    sib_short.wait()
    s_all[q] = s_own[...] + s_sib[...]
    to_chips(
        lambda chip: remote(s_all.at[q], s_all.at[q], red_send.at[3], red_recv.at[3], seq_dev(chip)).start()
    )

    wait_bytes(row_send.at[pl.ds(0, chips - 1)], red_recv.at[0])
    row_mid[yi, core] = jnp.sum(row_in[...], axis=0)

    def to_cross(r, carry):
        remote(
            row_mid.at[yi, core], row_mid.at[yi, core], red_send.at[1], red_recv.at[1], cross(r)
        ).start()
        return carry

    lax.fori_loop(1, 2 * y_size, to_cross, 0)

    wait_bytes(gp_send, ret_recv.at[1])
    gp32[...] = gp_ret[...].astype(F32).reshape(gp32.shape)
    for s in range(3):
        for cb in range(blocks):
            for j in range(ROWS):
                rows = pl.ds(cb * 8 * 3 * ROWS + s * ROWS + j, 8, stride=3 * ROWS)
                gp[s, cb * 8 : cb * 8 + 8, j * LANES : (j + 1) * LANES] = gp32[rows, :].astype(BF16)
    store_gp = pltpu.make_async_copy(gp, gp_out, store_sem.at[0])
    store_gp.start()

    mid_rest = row_in.at[pl.ds(0, 2 * y_size - 1)]
    wait_bytes(mid_rest, red_recv.at[1])
    pair = row_mid[yi, 0] + row_mid[yi, 1]
    every = row_mid[0, 0] + row_mid[0, 1]
    for y in range(1, y_size):
        every = every + (row_mid[y, 0] + row_mid[y, 1])
    scale = 1.0 / math.sqrt(length)
    row_all[q] = jnp.where(lane1 < units, pair, every) * scale
    to_chips(
        lambda chip: remote(row_all.at[q], row_all.at[q], red_send.at[2], red_recv.at[2], seq_dev(chip)).start()
    )
    wait_bytes(row_send.at[pl.ds(0, chips - 1)], red_recv.at[3])
    shorts = s_all[...].reshape(channels, LANES) * scale
    for s in range(3):
        short_rows[s] = jnp.concatenate(
            [as_row(shorts[:, 3 * s + j : 3 * s + j + 1]) for j in range(3)], 0
        )
    wait_bytes(row_send.at[pl.ds(0, chips - 1)], red_recv.at[2])
    rows = row_all[...].reshape(channels, LANES)
    small[0] = rows[:, :units]
    small[1] = rows[:, units:]
    stores = [
        pltpu.make_async_copy(small.at[0], fout_out, store_sem.at[1]),
        pltpu.make_async_copy(small.at[1], fin_out, store_sem.at[2]),
        pltpu.make_async_copy(short_rows, short_out, store_sem.at[3]),
    ]
    for copy in stores:
        copy.start()

    wait_bytes(raw_send.at[pl.ds(0, chips - 1)], in_send.at[0])
    wait_bytes(k_send.at[pl.ds(0, (chips - 1) * ROWS)], in_send.at[1])
    for slot, buf in ((0, kg_send), (1, gp_send)):
        wait_bytes(buf.at[pl.ds(0, chips - 1)], ret_send.at[slot])

        @pl.when(lax.div(me, chips) != core)
        def _():
            wait_bytes(buf.at[0], ret_send.at[slot])

    for slot in (0, 2, 3):
        wait_bytes(row_send.at[pl.ds(0, chips - 1)], red_send.at[slot])
    wait_bytes(mid_rest, red_send.at[1])
    store_gp.wait()
    for copy in stores:
        copy.wait()


def move_outputs(*refs):
    count = (len(refs) - 1) // 2
    copies = [pltpu.make_async_copy(refs[i], refs[count + i], refs[-1].at[i]) for i in range(count)]
    for copy in copies:
        copy.start()
    for copy in copies:
        copy.wait()


def shards(devices, y_size, tables, proj, cotangent, short_w, filter_in, filter_out, rates):
    channels = cotangent.shape[0]
    feats, order = filter_in.shape
    chips = devices // 2
    outer = devices * ROWS
    half = outer // 2
    hbm = pl.BlockSpec(memory_space=pltpu.HBM)
    dma = pltpu.SemaphoreType.DMA

    def f32(*shape):
        return pltpu.VMEM(shape, F32)

    def bf16(*shape):
        return pltpu.VMEM(shape, BF16)

    shapes = (
        jax.ShapeDtypeStruct(proj.shape, BF16),
        jax.ShapeDtypeStruct((3, 3, channels), F32),
        jax.ShapeDtypeStruct((channels, order), F32),
        jax.ShapeDtypeStruct((feats, order), F32),
    )
    results = pl.pallas_call(
        functools.partial(kernel, devices, y_size),
        out_shape=shapes,
        in_specs=[hbm] * 11,
        out_specs=(hbm,) * 4,
        scratch_shapes=[
            bf16(*proj.shape),
            bf16(*cotangent.shape),
            f32(3, 3, channels),
            f32(feats, order),
            f32(channels, order),
            f32(1, channels),
            bf16(2, outer, outer),
            bf16(2, outer, outer),
            f32(2, half, LANES),
            bf16(2, 2 * LANES, 2 * LANES),
            bf16(2, 2 * LANES, 2 * LANES),
            f32(feats, TOKENS),
            f32(order, TOKENS),
            f32(order, TOKENS),
            f32(channels, TOKENS),
            f32(chips * 4 * ROWS, LANES),
            bf16(chips, 4, ROWS, LANES),
            bf16(chips, 2, 4, ROWS, LANES),
            f32(chips * ROWS, LANES),
            f32(chips, 2, ROWS, LANES),
            f32(3, 2, outer, LANES),
            f32(2, outer, LANES),
            f32(3, half, 2 * LANES),
            f32(3, outer, LANES),
            f32(3, half + ROWS, LANES),
            f32(chips, ROWS, LANES),
            f32(chips, ROWS, LANES),
            f32(3, half + ROWS, LANES),
            bf16(chips, 3, ROWS, LANES),
            bf16(chips, 3, ROWS, LANES),
            f32(chips * 3 * ROWS, LANES),
            bf16(*proj.shape),
            f32(chips, 1, LANES),
            f32(chips, 1, LANES),
            f32(y_size, 2, 1, LANES),
            f32(chips, 1, LANES),
            f32(1, LANES),
            f32(1, LANES),
            f32(chips, 1, LANES),
            f32(2, channels, order),
            f32(3, 3, channels),
            dma((11,)), dma((2,)), dma((2,)), dma((3,)), dma((3,)), dma((2,)), dma((2,)), dma((2,)), dma((2,)),
            dma((4,)), dma((4,)), dma((4,)),
        ],
        compiler_params=pltpu.CompilerParams(
            collective_id=0, has_side_effects=True, vmem_limit_bytes=56 << 20
        ),
    )(proj, cotangent, short_w.transpose(0, 2, 1), filter_in, filter_out.T, rates.reshape(1, channels), *tables)
    grad_proj, grad_short, grad_out, grad_in = pl.pallas_call(
        move_outputs,
        out_shape=shapes,
        in_specs=[hbm] * 4,
        out_specs=(hbm,) * 4,
        scratch_shapes=[dma((4,))],
        compiler_params=pltpu.CompilerParams(vmem_limit_bytes=56 << 20),
    )(*results)
    return grad_proj, grad_short.transpose(0, 2, 1), grad_out.T, grad_in


def solution(mesh):
    devices, y_size = mesh.shape["seq"], mesh.shape["ch"]
    tables = make_tables(devices)

    def run(*args):
        return shards(devices, y_size, [jnp.asarray(t) for t in tables], *args)

    return jax.shard_map(
        run,
        mesh=mesh,
        in_specs=(
            P(None, "ch", "seq"),
            P("ch", "seq"),
            P(None, "ch", None),
            P(),
            P(None, "ch"),
            P("ch"),
        ),
        out_specs=(P(None, "ch", "seq"), P(None, "ch", None), P(None, "ch"), P()),
        check_vma=False,
    )
```

time: 65.3 us -> 61.6 us (0.943)
  local copies, waits for them, and re-layouts: 5.55 us -> 0 us
  Pallas kernels: 58.7 us -> 60.8 us
    unnamed x4 -> x0, local copies, waits for them, and re-layouts: 5.55 us -> none
    pallas_call x1 -> x2, Pallas kernels: 58.7 us -> 60.8 us  [the longest x1 52.5 us: shards(): pl.pallas_call(functools.partial(kernel, devices, y_size), out_shape=shap...]
where the time goes in v3:
time: 61.6 us; the launch traced here: 61.4 us
  Pallas kernels  60.8 us (99%)
  between operations  0.64 us (1%)
    pallas_call x1, Pallas kernels, shards(): pl.pallas_call(functools.partial(kernel, devices, y_size), out_shape=shap...  52.5 us
    pallas_call x1, Pallas kernels, shards(): pl.pallas_call(move_outputs, out_shape=shapes, in_specs=[hbm] * 4, out_sp...  8.23 us

profile of v3, /device:TPU:1, one launch (start us, length us, event | category | flops | bytes accessed | tf_op | source)
XLA Modules:
  0.0 61.4 jit_solution(1011056839445319774)
XLA Ops:
  0.6 52.5 %shard_map.138 = (bf16[3,32,1024]{2,1,0:T(8,128)(2,1)}, f32[3,3,32]{2,1,0:T(4,128)}, f32[32,64]{1,0:T(8,128)}, f32[32,64]{1,0:T(8,128)}) custom-call(bf16[3,32,1024]{2,1,0:T(8,128)(2,1)} %proj_hbm.1, bf16[32,1024]{1,0:T(8,128)(2,1)} %cot_hbm.1, f32[3,3,32]{2,1,0:T(4,128)} %bitcast.6, f32[32,64]{1,0:T(8,128)} %fin_hbm.1, f32[32,64]{1,0:T(8,128)} %bitcast.5, ...), custom_call_target="tpu_custom_call" | custom-call | tf_op jit(solution)/shard_map/pallas_call | solution.py:503
  53.2 8.2 %shard_map.139 = (bf16[3,32,1024]{2,1,0:T(8,128)(2,1)}, f32[3,3,32]{2,1,0:T(4,128)}, f32[32,64]{1,0:T(8,128)}, f32[32,64]{1,0:T(8,128)}) custom-call(bf16[3,32,1024]{2,1,0:T(8,128)(2,1)} %get-tuple-element.12.refs_0_, f32[3,3,32]{2,1,0:T(4,128)} %get-tuple-element.13.refs_1_, f32[32,64]{1,0:T(8,128)} %get-tuple-element.14.refs_2_, ...), custom_call_target="tpu_custom_call" | custom-call | tf_op jit(solution)/shard_map/pallas_call | solution.py:557

commit v4 on v3

--- a/solution.py
+++ b/solution.py
@@ -17,6 +17,7 @@
 LANES = 128
 ROWS = 8
 TOKENS = ROWS * LANES
+Z_SIZE = 8
 
 
 def bf16_pair(table):
@@ -107,12 +108,12 @@
     return high, (x - high.astype(F32)).astype(BF16)
 
 
-def dot_one(a, b):
-    return lax.dot_general(a, b, (((1,), (0,)), ((), ())), preferred_element_type=F32)
-
-
-def dot3(a, b):
-    return dot_one(a[0], b[0]) + (dot_one(a[0], b[1]) + dot_one(a[1], b[0]))
+def dot_one(a, b, da=1, db=0):
+    return lax.dot_general(a, b, (((da,), (db,)), ((), ())), preferred_element_type=F32)
+
+
+def dot3(a, b, da=1, db=0):
+    return dot_one(a[0], b[0], da, db) + (dot_one(a[0], b[1], da, db) + dot_one(a[1], b[0], da, db))
 
 
 def dot_exact(a, b, dims):
@@ -122,12 +123,12 @@
 def kernel(
     devices, y_size,
     proj_hbm, cot_hbm, sw_hbm, fin_hbm, fout_hbm, rates_hbm, f1_hbm, f1t_hbm, tw_hbm, f2_hbm, f2t_hbm,
-    gp_out, short_out, fout_out, fin_out,
+    gp, small,
     proj, cot, sw, fin, fout, rates, f1, f1t, tw, f2, f2t,
-    feat, hid, hcos, env, raw32, raw_send, raw, k_send, kbuf, shifts, kv, spec, ybuf, xb, kg_send, kg_ret,
-    res, gp_send, gp_ret, gp32, gp, row_send, row_in, row_mid, row_all, s_own, s_sib, s_all, small, short_rows,
-    load_sem, in_send, in_recv, sib_send, sib_recv, x_send, x_recv, ret_send, ret_recv,
-    red_send, red_recv, store_sem,
+    feat, hcos, env, raw32, raw_send, raw, k_send, kbuf, shifts, kv, spec, ybuf, xb, kg_send, kg_ret,
+    res, gp_send, gp_ret, gp32, hid2, feat2, r_own, r_sib, r_z, r_xy, r_all, s_own, s_sib, s_all,
+    load_sem, in_send, in_recv, raw_recv, sib_send, sib_recv, x_send, x_recv, ret_send, ret_recv,
+    red_send, red_recv,
 ):
     chips = devices // 2
     channels = cot.shape[0]
@@ -136,7 +137,7 @@
     half = outer // 2
     local = half + ROWS
     blocks = channels // 8
-    units = hid.shape[0]
+    units = hcos.shape[0]
     me = lax.axis_index("seq")
     yi = lax.axis_index("ch")
     q = lax.div(me, 2)
@@ -148,29 +149,36 @@
 
     barrier = pltpu.get_barrier_semaphore()
 
-    def greet(r, carry):
-        pl.semaphore_signal(barrier, inc=1, device_id={"seq": lax.rem(me + r, devices)}, device_id_type=MESH)
-        return carry
-
-    lax.fori_loop(1, devices, greet, 0)
-
-    def cross(r):
-        y = lax.rem(yi + lax.div(r, 2), y_size)
-        return {"ch": y, "seq": 2 * q + lax.rem(core + r, 2)}
-
-    def greet_y(r, carry):
-        pl.semaphore_signal(barrier, inc=1, device_id=cross(r), device_id_type=MESH)
-        return carry
-
-    lax.fori_loop(2, 2 * y_size, greet_y, 0)
-
+    order = (3, 4, 0, 1, 2, 5, 6, 7, 8, 9, 10)
     moves = (
         (fin_hbm, fin), (rates_hbm, rates), (fout_hbm, fout), (proj_hbm, proj), (cot_hbm, cot), (sw_hbm, sw),
         (f1_hbm.at[core], f1), (tw_hbm.at[core], tw), (f2_hbm, f2), (f2t_hbm, f2t), (f1t_hbm.at[core], f1t),
     )
     loads = [pltpu.make_async_copy(src, dst, load_sem.at[i]) for i, (src, dst) in enumerate(moves)]
-    for copy in loads:
-        copy.start()
+    for i in order[:2]:
+        loads[i].start()
+
+    x_size = chips // Z_SIZE
+    xi = lax.div(q, Z_SIZE)
+    zi = lax.rem(q, Z_SIZE)
+
+    def cross(r):
+        x = lax.rem(xi + lax.div(r, y_size), x_size)
+        return {"ch": lax.rem(yi + lax.rem(r, y_size), y_size), "seq": 2 * (x * Z_SIZE + zi) + core}
+
+    def greet(r, carry):
+        pl.semaphore_signal(barrier, inc=1, device_id=seq_dev(lax.rem(q + r, chips)), device_id_type=MESH)
+        return carry
+
+    def greet_cross(r, carry):
+        pl.semaphore_signal(barrier, inc=1, device_id=cross(r), device_id_type=MESH)
+        return carry
+
+    lax.fori_loop(1, chips, greet, 0)
+    pl.semaphore_signal(barrier, inc=1, device_id={"seq": sib}, device_id_type=MESH)
+    lax.fori_loop(1, x_size * y_size, greet_cross, 0)
+    for i in order[2:]:
+        loads[i].start()
 
     def remote(src, dst, send_sem, recv_sem, device):
         return pltpu.make_async_remote_copy(
@@ -180,13 +188,7 @@
     def wait_bytes(part, sem):
         pltpu.make_async_copy(part, part, sem).wait()
 
-    row = lax.broadcasted_iota(jnp.int32, feat.shape, 0)
-    position = me * TOKENS + lax.broadcasted_iota(jnp.int32, feat.shape, 1)
-    odd = row & 1
-    phase = position * (1 + (row >> 1) * 499) - odd * (length // 4) + length // 2
-    phase = (phase & (length - 1)) - length // 2
-    feat[...] = sin_small((length // 4 - jnp.abs(phase)).astype(F32) * (2.0 * math.pi / length))
-    for copy in loads[:5]:
+    for copy in loads[3:5]:
         copy.wait()
 
     for s in range(4):
@@ -197,42 +199,46 @@
                 raw32[rows, :] = value[cb * 8 : cb * 8 + 8, j * LANES : (j + 1) * LANES]
     raw_send[...] = raw32[...].reshape(raw_send.shape).astype(BF16)
 
+    pl.semaphore_wait(barrier, chips + x_size * y_size - 1)
+
+    def rows_of(chip):
+        return pl.ds(pl.multiple_of(chip * ROWS, ROWS), ROWS)
+
+    def to_chips(start):
+        def one(r, carry):
+            start(lax.rem(q + r, chips))
+            return carry
+
+        lax.fori_loop(1, chips, one, 0)
+
+    to_chips(
+        lambda chip: remote(
+            raw_send.at[chip], raw.at[q, core], in_send.at[0], raw_recv.at[q], seq_dev(chip)
+        ).start()
+    )
+    raw[q, core] = raw_send[q]
+
+    row = lax.broadcasted_iota(jnp.int32, feat.shape, 0)
+    position = me * TOKENS + lax.broadcasted_iota(jnp.int32, feat.shape, 1)
+    odd = row & 1
+    phase = position * (1 + (row >> 1) * 499) - odd * (length // 4) + length // 2
+    phase = (phase & (length - 1)) - length // 2
+    feat[...] = sin_small((length // 4 - jnp.abs(phase)).astype(F32) * (2.0 * math.pi / length))
+    for copy in loads[:3]:
+        copy.wait()
+
     preact = dot_exact(fin[...], feat[...], ((0,), (0,)))
     sine, cosine = sin_cos(preact)
-    hid[...] = sine
+    hid2[0], hid2[1] = split(sine)
+    feat2[0], feat2[1] = split(feat[...])
     hcos[...] = cosine
     relative = (me * TOKENS + lax.broadcasted_iota(jnp.int32, env.shape, 1)).astype(F32) * (1.0 / length)
     rate = column(rates[...])
     env[...] = jnp.exp(-rate * relative) * inverse_spread(rate, length)
-    filt = env[...] * dot_exact(fout[...], hid[...], ((1,), (0,)))
+    filt = env[...] * dot3(split(fout[...]), (hid2[0], hid2[1]))
     for cb in range(blocks):
         for j in range(ROWS):
             k_send[pl.ds(cb * 64 + j, 8, stride=8), :] = filt[cb * 8 : cb * 8 + 8, j * LANES : (j + 1) * LANES]
-
-    pl.semaphore_wait(barrier, devices - 1 + 2 * y_size - 2)
-
-    def rows_of(chip):
-        return pl.ds(pl.multiple_of(chip * ROWS, ROWS), ROWS)
-
-    def to_chips(start):
-        def one(r, carry):
-            start(lax.rem(q + r, chips))
-            return carry
-
-        lax.fori_loop(1, chips, one, 0)
-
-    to_chips(
-        lambda chip: remote(
-            raw_send.at[chip], raw.at[q, core], in_send.at[0], in_recv.at[0], seq_dev(chip)
-        ).start()
-    )
-    raw[q, core] = raw_send[q]
-    to_chips(
-        lambda chip: remote(
-            k_send.at[rows_of(chip)], kbuf.at[q, core], in_send.at[1], in_recv.at[1], seq_dev(chip)
-        ).start()
-    )
-    kbuf[q, core] = k_send[rows_of(q)]
 
     for copy in loads[5:]:
         copy.wait()
@@ -242,10 +248,25 @@
         for s in range(3)
     ]
 
-    wait_bytes(raw_send.at[pl.ds(0, chips - 1)], in_recv.at[0])
-    sib_raw = remote(raw.at[:, core], raw.at[:, core], sib_send.at[0], sib_recv.at[0], {"seq": sib})
-    sib_raw.start()
-    sib_raw.wait()
+    def hand_on(chip):
+        remote(raw.at[chip, core], raw.at[chip, core], sib_send.at[0], sib_recv.at[0], {"seq": sib}).start()
+
+    def arrived(r, carry):
+        chip = lax.rem(q + chips - r, chips)
+        pltpu.make_async_copy(raw.at[chip, core], raw.at[chip, core], raw_recv.at[chip]).wait()
+        hand_on(chip)
+        return carry
+
+    hand_on(q)
+    lax.fori_loop(1, chips // 2, arrived, 0)
+    to_chips(
+        lambda chip: remote(
+            k_send.at[rows_of(chip)], kbuf.at[q, core], in_send.at[1], in_recv.at[1], seq_dev(chip)
+        ).start()
+    )
+    kbuf[q, core] = k_send[rows_of(q)]
+    lax.fori_loop(chips // 2, chips, arrived, 0)
+    wait_bytes(raw_send, sib_recv.at[0])
 
     lane = lax.broadcasted_iota(jnp.int32, (outer, LANES), 1)
     line = lax.broadcasted_iota(jnp.int32, (outer, LANES), 0)
@@ -375,6 +396,12 @@
     sib_short = remote(s_own, s_sib, sib_send.at[2], sib_recv.at[2], {"seq": sib})
     sib_short.start()
 
+    sib_short.wait()
+    s_all[q] = s_own[...] + s_sib[...]
+    to_chips(
+        lambda chip: remote(s_all.at[q], s_all.at[q], red_send.at[4], red_recv.at[4], seq_dev(chip)).start()
+    )
+
     wait_bytes(kg_send, ret_recv.at[0])
     weighted = env[...] * jnp.concatenate(
         [
@@ -386,33 +413,22 @@
             for cb in range(blocks)
         ], 0,
     )
-    out_part = dot_exact(weighted, hid[...], ((1,), (1,)))
-    grad_hidden = dot_exact(fout[...], weighted, ((0,), (0,))) * hcos[...]
-    in_part = dot_exact(feat[...], grad_hidden, ((1,), (1,)))
-    row_send[...] = jnp.concatenate([out_part, in_part], 1).reshape(row_send.shape)
-    to_chips(
-        lambda chip: remote(
-            row_send.at[chip], row_in.at[q], red_send.at[0], red_recv.at[0], seq_dev(chip)
-        ).start()
-    )
-    row_in[q] = row_send[q]
-
-    sib_short.wait()
-    s_all[q] = s_own[...] + s_sib[...]
-    to_chips(
-        lambda chip: remote(s_all.at[q], s_all.at[q], red_send.at[3], red_recv.at[3], seq_dev(chip)).start()
-    )
-
-    wait_bytes(row_send.at[pl.ds(0, chips - 1)], red_recv.at[0])
-    row_mid[yi, core] = jnp.sum(row_in[...], axis=0)
-
-    def to_cross(r, carry):
-        remote(
-            row_mid.at[yi, core], row_mid.at[yi, core], red_send.at[1], red_recv.at[1], cross(r)
-        ).start()
+    pair = split(weighted)
+    out_part = dot3(pair, (hid2[0], hid2[1]), 1, 1)
+    grad_hidden = dot3(split(fout[...]), pair, 0, 0) * hcos[...]
+    in_part = dot3((feat2[0], feat2[1]), split(grad_hidden), 1, 1)
+    r_own[...] = jnp.concatenate([out_part, in_part], 1).reshape(r_own.shape)
+    red_core = remote(r_own.at[1 - core], r_sib, red_send.at[0], red_recv.at[0], {"seq": sib})
+    red_core.start()
+    red_core.wait()
+    r_z[zi] = r_own[core] + r_sib[...]
+
+    def to_z(r, carry):
+        device = seq_dev(xi * Z_SIZE + lax.rem(zi + r, Z_SIZE))
+        remote(r_z.at[zi], r_z.at[zi], red_send.at[1], red_recv.at[1], device).start()
         return carry
 
-    lax.fori_loop(1, 2 * y_size, to_cross, 0)
+    lax.fori_loop(1, Z_SIZE, to_z, 0)
 
     wait_bytes(gp_send, ret_recv.at[1])
     gp32[...] = gp_ret[...].astype(F32).reshape(gp32.shape)
@@ -421,37 +437,46 @@
             for j in range(ROWS):
                 rows = pl.ds(cb * 8 * 3 * ROWS + s * ROWS + j, 8, stride=3 * ROWS)
                 gp[s, cb * 8 : cb * 8 + 8, j * LANES : (j + 1) * LANES] = gp32[rows, :].astype(BF16)
-    store_gp = pltpu.make_async_copy(gp, gp_out, store_sem.at[0])
-    store_gp.start()
-
-    mid_rest = row_in.at[pl.ds(0, 2 * y_size - 1)]
-    wait_bytes(mid_rest, red_recv.at[1])
-    pair = row_mid[yi, 0] + row_mid[yi, 1]
-    every = row_mid[0, 0] + row_mid[0, 1]
+
+    z_rest = r_z.at[pl.ds(0, Z_SIZE - 1)]
+    wait_bytes(z_rest, red_recv.at[1])
+    total = r_z[0]
+    for i in range(1, Z_SIZE):
+        total = total + r_z[i]
+    here = xi * y_size + yi
+    r_xy[here] = total
+
+    def to_cross(r, carry):
+        remote(r_xy.at[here], r_xy.at[here], red_send.at[2], red_recv.at[2], cross(r)).start()
+        return carry
+
+    lax.fori_loop(1, x_size * y_size, to_cross, 0)
+
+    scale = 1.0 / math.sqrt(length)
+    wait_bytes(s_all.at[pl.ds(0, chips - 1)], red_recv.at[4])
+    shorts = s_all[...].reshape(channels, LANES) * scale
+    for at in range(9):
+        small[channels + at : channels + at + 1, 0:channels] = as_row(shorts[:, at : at + 1])
+
+    def wait_cross(sem):
+        wait_bytes(r_xy.at[pl.ds(0, x_size * y_size - 1)], sem)
+
+    wait_cross(red_recv.at[2])
+    columns = []
+    for y in [yi] + list(range(y_size)):
+        column_sum = r_xy[y]
+        for x in range(1, x_size):
+            column_sum = column_sum + r_xy[x * y_size + y]
+        columns.append(column_sum)
+    every = columns[1]
     for y in range(1, y_size):
-        every = every + (row_mid[y, 0] + row_mid[y, 1])
-    scale = 1.0 / math.sqrt(length)
-    row_all[q] = jnp.where(lane1 < units, pair, every) * scale
-    to_chips(
-        lambda chip: remote(row_all.at[q], row_all.at[q], red_send.at[2], red_recv.at[2], seq_dev(chip)).start()
-    )
-    wait_bytes(row_send.at[pl.ds(0, chips - 1)], red_recv.at[3])
-    shorts = s_all[...].reshape(channels, LANES) * scale
-    for s in range(3):
-        short_rows[s] = jnp.concatenate(
-            [as_row(shorts[:, 3 * s + j : 3 * s + j + 1]) for j in range(3)], 0
-        )
-    wait_bytes(row_send.at[pl.ds(0, chips - 1)], red_recv.at[2])
-    rows = row_all[...].reshape(channels, LANES)
-    small[0] = rows[:, :units]
-    small[1] = rows[:, units:]
-    stores = [
-        pltpu.make_async_copy(small.at[0], fout_out, store_sem.at[1]),
-        pltpu.make_async_copy(small.at[1], fin_out, store_sem.at[2]),
-        pltpu.make_async_copy(short_rows, short_out, store_sem.at[3]),
-    ]
-    for copy in stores:
-        copy.start()
+        every = every + columns[1 + y]
+    lanes = lax.broadcasted_iota(jnp.int32, every.shape, 1)
+    r_all[core] = jnp.where(lanes < units, columns[0], every) * scale
+    red_back = remote(r_all.at[core], r_all.at[core], red_send.at[3], red_recv.at[3], {"seq": sib})
+    red_back.start()
+    red_back.wait()
+    small[0:channels, :] = r_all[...].reshape(channels, LANES)
 
     wait_bytes(raw_send.at[pl.ds(0, chips - 1)], in_send.at[0])
     wait_bytes(k_send.at[pl.ds(0, (chips - 1) * ROWS)], in_send.at[1])
@@ -462,21 +487,10 @@
         def _():
             wait_bytes(buf.at[0], ret_send.at[slot])
 
-    for slot in (0, 2, 3):
-        wait_bytes(row_send.at[pl.ds(0, chips - 1)], red_send.at[slot])
-    wait_bytes(mid_rest, red_send.at[1])
-    store_gp.wait()
-    for copy in stores:
-        copy.wait()
-
-
-def move_outputs(*refs):
-    count = (len(refs) - 1) // 2
-    copies = [pltpu.make_async_copy(refs[i], refs[count + i], refs[-1].at[i]) for i in range(count)]
-    for copy in copies:
-        copy.start()
-    for copy in copies:
-        copy.wait()
+    wait_bytes(raw_send, sib_send.at[0])
+    wait_bytes(z_rest, red_send.at[1])
+    wait_cross(red_send.at[2])
+    wait_bytes(s_all.at[pl.ds(0, chips - 1)], red_send.at[4])
 
 
 def shards(devices, y_size, tables, proj, cotangent, short_w, filter_in, filter_out, rates):
@@ -494,17 +508,17 @@
     def bf16(*shape):
         return pltpu.VMEM(shape, BF16)
 
-    shapes = (
-        jax.ShapeDtypeStruct(proj.shape, BF16),
-        jax.ShapeDtypeStruct((3, 3, channels), F32),
-        jax.ShapeDtypeStruct((channels, order), F32),
-        jax.ShapeDtypeStruct((feats, order), F32),
-    )
-    results = pl.pallas_call(
+    operands = (
+        proj, cotangent, short_w.transpose(0, 2, 1), filter_in, filter_out.T, rates.reshape(1, channels), *tables
+    )
+    grad_proj, small = pl.pallas_call(
         functools.partial(kernel, devices, y_size),
-        out_shape=shapes,
+        out_shape=(
+            jax.ShapeDtypeStruct(proj.shape, BF16),
+            jax.ShapeDtypeStruct((channels + 16, LANES), F32),
+        ),
         in_specs=[hbm] * 11,
-        out_specs=(hbm,) * 4,
+        out_specs=(pl.BlockSpec(memory_space=pltpu.VMEM),) * 2,
         scratch_shapes=[
             bf16(*proj.shape),
             bf16(*cotangent.shape),
@@ -518,7 +532,6 @@
             bf16(2, 2 * LANES, 2 * LANES),
             bf16(2, 2 * LANES, 2 * LANES),
             f32(feats, TOKENS),
-            f32(order, TOKENS),
             f32(order, TOKENS),
             f32(channels, TOKENS),
             f32(chips * 4 * ROWS, LANES),
@@ -537,32 +550,25 @@
             bf16(chips, 3, ROWS, LANES),
             bf16(chips, 3, ROWS, LANES),
             f32(chips * 3 * ROWS, LANES),
-            bf16(*proj.shape),
-            f32(chips, 1, LANES),
-            f32(chips, 1, LANES),
-            f32(y_size, 2, 1, LANES),
-            f32(chips, 1, LANES),
+            bf16(2, order, TOKENS),
+            bf16(2, feats, TOKENS),
+            f32(2, channels // 2, LANES),
+            f32(channels // 2, LANES),
+            f32(Z_SIZE, channels // 2, LANES),
+            f32(chips // Z_SIZE * y_size, channels // 2, LANES),
+            f32(2, channels // 2, LANES),
             f32(1, LANES),
             f32(1, LANES),
             f32(chips, 1, LANES),
-            f32(2, channels, order),
-            f32(3, 3, channels),
-            dma((11,)), dma((2,)), dma((2,)), dma((3,)), dma((3,)), dma((2,)), dma((2,)), dma((2,)), dma((2,)),
-            dma((4,)), dma((4,)), dma((4,)),
+            dma((11,)), dma((2,)), dma((2,)), dma((chips,)), dma((3,)), dma((3,)), dma((2,)), dma((2,)),
+            dma((2,)), dma((2,)), dma((5,)), dma((5,)),
         ],
         compiler_params=pltpu.CompilerParams(
-            collective_id=0, has_side_effects=True, vmem_limit_bytes=56 << 20
+            collective_id=0, has_side_effects=True, vmem_limit_bytes=32 << 20
         ),
-    )(proj, cotangent, short_w.transpose(0, 2, 1), filter_in, filter_out.T, rates.reshape(1, channels), *tables)
-    grad_proj, grad_short, grad_out, grad_in = pl.pallas_call(
-        move_outputs,
-        out_shape=shapes,
-        in_specs=[hbm] * 4,
-        out_specs=(hbm,) * 4,
-        scratch_shapes=[dma((4,))],
-        compiler_params=pltpu.CompilerParams(vmem_limit_bytes=56 << 20),
-    )(*results)
-    return grad_proj, grad_short.transpose(0, 2, 1), grad_out.T, grad_in
+    )(*[pltpu.with_memory_space_constraint(x, pltpu.HBM) for x in operands])
+    grad_short = small[channels : channels + 9, :channels].reshape(3, 3, channels).transpose(0, 2, 1)
+    return grad_proj, grad_short, small[:channels, :order].T, small[:feats, order:]
 
 
 def solution(mesh):

time: 61.6 us -> 51 us (0.83)
  Pallas kernels: 60.8 us -> 48.3 us
  local copies, waits for them, and re-layouts: 0 us -> 1.96 us
    pallas_call x2 -> x1, Pallas kernels: 60.8 us -> 48.3 us  [shards(): pl.pallas_call(functools.partial(kernel, devices, y_size), out_shape=(jax...]
    slice x0 -> x2, local copies, waits for them, and re-layouts: none -> 0.68 us  [the longest x1 0.68 us: shards(): small[:feats, order:]]
    unnamed x0 -> x1, local copies, waits for them, and re-layouts: none -> 0.68 us
where the time goes in v4:
time: 51 us
  Pallas kernels  48.3 us (95%)
  local copies, waits for them, and re-layouts  1.96 us (4%)
  between operations  0.65 us (1%)
    pallas_call x1, Pallas kernels, shards(): pl.pallas_call(functools.partial(kernel, devices, y_size), out_shape=(jax...  48.3 us

profile of v4, /device:TPU:1, one launch (start us, length us, event | category | flops | bytes accessed | tf_op | source)
XLA Modules:
  0.0 51.0 jit_solution(16990304364187237581)
XLA Ops:
  0.6 48.3 %shard_map.138 = (bf16[3,32,1024]{2,1,0:T(8,128)(2,1)S(1)}, f32[48,128]{1,0:T(8,128)S(1)}) custom-call(bf16[3,32,1024]{2,1,0:T(8,128)(2,1)} %proj_hbm.1, bf16[32,1024]{1,0:T(8,128)(2,1)} %cot_hbm.1, f32[3,3,32]{2,1,0:T(4,128)} %bitcast.7, f32[32,64]{1,0:T(8,128)} %fin_hbm.1, f32[32,64]{1,0:T(8,128)} %bitcast.6, f32[1,32]{1,0:T(1,128)} %bitcast.9, ...), custom_call_target="tpu_custom_call" | custom-call | tf_op jit(solution)/shard_map/pallas_call | solution.py:514
  49.0 0.6 %reshape.15 = f32[3,3,32]{2,1,0:T(4,128)} reshape(f32[9,32]{1,0:T(8,128)S(1)} %slice.9) | data formatting | bytes 2304 | tf_op jit(solution)/shard_map/reshape | solution.py:570
  49.6 0.7 %fusion = (f32[32,64]{1,0:T(8,128)}, f32[64,32]{0,1:T(8,128)}) fusion(f32[48,128]{1,0:T(8,128)S(1)} %get-tuple-element.7), kind=kLoop, calls=%fused_computation.1 | loop fusion | bytes 32768 | tf_op jit(solution)/shard_map/slice | solution.py:571
  50.3 0.7 %copy.16 = bf16[3,32,1024]{2,1,0:T(8,128)(2,1)} copy(bf16[3,32,1024]{2,1,0:T(8,128)(2,1)S(1)} %get-tuple-element.14) | data formatting | bytes 393216
  (1 shorter events, 0.0 us)

commit v5 on v4

--- a/solution.py
+++ b/solution.py
@@ -18,6 +18,7 @@
 ROWS = 8
 TOKENS = ROWS * LANES
 Z_SIZE = 8
+EXTRA = 16
 
 
 def bf16_pair(table):
@@ -38,7 +39,9 @@
         angle = num * (2.0 * np.pi / (4 * outer))
         matrix = np.concatenate([np.cos(angle), -np.sin(angle)], 0)
         fwd.append(bf16_pair(matrix))
-        back.append(bf16_pair(np.ascontiguousarray(matrix.T)))
+        starts = [(1 - core) * (half - EXTRA), core * (half - EXTRA)]
+        rows = np.concatenate([start + np.arange(half + EXTRA) for start in starts])
+        back.append(bf16_pair(np.ascontiguousarray(matrix.T[rows])))
         num = (np.arange(LANES)[None, :] * (4 * k1[:, None] + 1)) % (4 * length)
         angle = num * (2.0 * np.pi / (4 * length))
         twiddle.append(np.stack([np.cos(angle), -np.sin(angle)]).astype(np.float32))
@@ -113,7 +116,9 @@
 
 
 def dot3(a, b, da=1, db=0):
-    return dot_one(a[0], b[0], da, db) + (dot_one(a[0], b[1], da, db) + dot_one(a[1], b[0], da, db))
+    return dot_one(
+        jnp.concatenate([a[0], a[0], a[1]], da), jnp.concatenate([b[0], b[1], b[0]], db), da, db
+    )
 
 
 def dot_exact(a, b, dims):
@@ -123,10 +128,10 @@
 def kernel(
     devices, y_size,
     proj_hbm, cot_hbm, sw_hbm, fin_hbm, fout_hbm, rates_hbm, f1_hbm, f1t_hbm, tw_hbm, f2_hbm, f2t_hbm,
-    gp, small,
+    gp, short_rows, fout_out, fin_out,
     proj, cot, sw, fin, fout, rates, f1, f1t, tw, f2, f2t,
-    feat, hcos, env, raw32, raw_send, raw, k_send, kbuf, shifts, kv, spec, ybuf, xb, kg_send, kg_ret,
-    res, gp_send, gp_ret, gp32, hid2, feat2, r_own, r_sib, r_z, r_xy, r_all, s_own, s_sib, s_all,
+    feat, hcos, env, raw32, raw_send, raw, k_send, kbuf, shifts, kv, spec, ybuf, yown, xb, kg_send, kg_ret,
+    res, gp_send, gp_ret, gp32, hid2, feat2, r_own, r_sib, r_z, r_x, r_xy, s_own, s_sib, s_all,
     load_sem, in_send, in_recv, raw_recv, sib_send, sib_recv, x_send, x_recv, ret_send, ret_recv,
     red_send, red_recv,
 ):
@@ -135,7 +140,7 @@
     length = devices * TOKENS
     outer = devices * ROWS
     half = outer // 2
-    local = half + ROWS
+    local = half + EXTRA
     blocks = channels // 8
     units = hcos.shape[0]
     me = lax.axis_index("seq")
@@ -155,16 +160,14 @@
         (f1_hbm.at[core], f1), (tw_hbm.at[core], tw), (f2_hbm, f2), (f2t_hbm, f2t), (f1t_hbm.at[core], f1t),
     )
     loads = [pltpu.make_async_copy(src, dst, load_sem.at[i]) for i, (src, dst) in enumerate(moves)]
-    for i in order[:2]:
-        loads[i].start()
-
     x_size = chips // Z_SIZE
     xi = lax.div(q, Z_SIZE)
     zi = lax.rem(q, Z_SIZE)
 
     def cross(r):
-        x = lax.rem(xi + lax.div(r, y_size), x_size)
-        return {"ch": lax.rem(yi + lax.rem(r, y_size), y_size), "seq": 2 * (x * Z_SIZE + zi) + core}
+        x = lax.rem(xi + lax.rem(lax.div(r, y_size), x_size), x_size)
+        other = lax.rem(core + lax.div(r, x_size * y_size), 2)
+        return {"ch": lax.rem(yi + lax.rem(r, y_size), y_size), "seq": 2 * (x * Z_SIZE + zi) + other}
 
     def greet(r, carry):
         pl.semaphore_signal(barrier, inc=1, device_id=seq_dev(lax.rem(q + r, chips)), device_id_type=MESH)
@@ -175,9 +178,8 @@
         return carry
 
     lax.fori_loop(1, chips, greet, 0)
-    pl.semaphore_signal(barrier, inc=1, device_id={"seq": sib}, device_id_type=MESH)
-    lax.fori_loop(1, x_size * y_size, greet_cross, 0)
-    for i in order[2:]:
+    lax.fori_loop(1, 2 * x_size * y_size, greet_cross, 0)
+    for i in order:
         loads[i].start()
 
     def remote(src, dst, send_sem, recv_sem, device):
@@ -199,7 +201,7 @@
                 raw32[rows, :] = value[cb * 8 : cb * 8 + 8, j * LANES : (j + 1) * LANES]
     raw_send[...] = raw32[...].reshape(raw_send.shape).astype(BF16)
 
-    pl.semaphore_wait(barrier, chips + x_size * y_size - 1)
+    pl.semaphore_wait(barrier, chips - 1 + 2 * x_size * y_size - 1)
 
     def rows_of(chip):
         return pl.ds(pl.multiple_of(chip * ROWS, ROWS), ROWS)
@@ -302,72 +304,80 @@
         zr, zi = z[:, :LANES], z[:, LANES:]
         return jnp.concatenate([zr * tw[0] + zi * tw[1], zi * tw[0] - zr * tw[1]], 0)
 
-    def finish(slots, columns):
-        y = dot3((f1t[0], f1t[1]), split(jnp.concatenate(columns, 1) if len(columns) > 1 else columns[0]))
-        for at, s in enumerate(slots):
-            ybuf[s] = y[:, at * LANES : (at + 1) * LANES]
-
-    mine = pl.ds(pl.multiple_of(core * (half - ROWS), ROWS), local)
-    theirs = pl.ds(pl.multiple_of((1 - core) * (half - ROWS), ROWS), local)
+    mine = pl.ds(pl.multiple_of(core * (half - EXTRA), ROWS), local)
+
+    def finish(slots, columns, exchange):
+        right = split(jnp.concatenate(columns, 1) if len(columns) > 1 else columns[0])
+        for own in (False, True):
+            rows = slice(local, 2 * local) if own else slice(0, local)
+            y = dot3((f1t[0, rows, :], f1t[1, rows, :]), right)
+            for at, s in enumerate(slots):
+                (yown if own else ybuf)[s] = y[:, at * LANES : (at + 1) * LANES]
+            if not own:
+                exchange.start()
 
     def swap(lo, hi, slot):
         return remote(
-            ybuf.at[lo:hi, theirs], xb.at[lo:hi], x_send.at[slot], x_recv.at[slot], {"seq": sib}
+            ybuf.at[lo:hi], xb.at[lo:hi], x_send.at[slot], x_recv.at[slot], {"seq": sib}
         )
 
     forward([gated, grad_conv], [1, 2])
     gr, gi = parts(1)
     dr, di = parts(2)
-    finish([0], [inverse_rows(dr * gr + di * gi, di * gr - dr * gi)])
     swap_k = swap(0, 1, 0)
-    swap_k.start()
+    finish([0], [inverse_rows(dr * gr + di * gi, di * gr - dr * gi)], swap_k)
+
+    is_local = lax.div(me, chips) == core
+
+    def send_half(src, dst, slot, first, end):
+        at = lax.rem(me, chips)
+
+        def one(r, carry):
+            d = lax.rem(at + r, chips)
+            device = {"seq": core * chips + d}
+            remote(src.at[d], dst.at[q], ret_send.at[slot], ret_recv.at[slot], device).start()
+            return carry
+
+        lax.fori_loop(max(first, 1), end, one, 0)
+        if first == 0:
+
+            @pl.when(is_local)
+            def _():
+                pltpu.make_async_copy(src.at[at], dst.at[q], ret_recv.at[slot]).start()
+
+            @pl.when(jnp.logical_not(is_local))
+            def _():
+                one(0, 0)
+
+    swap_k.wait()
+    own_rows = pl.ds(pl.multiple_of(core * EXTRA, ROWS), half)
+    kg = (yown[0, own_rows, :] + xb[0, own_rows, :]) * (1.0 / length)
+    kg_send[...] = kg.reshape(kg_send.shape)
+    send_half(kg_send, kg_ret, 0, 0, chips)
 
     wait_bytes(k_send.at[pl.ds(0, (chips - 1) * ROWS)], in_recv.at[1])
     sib_k = remote(kbuf.at[:, core], kbuf.at[:, core], sib_send.at[1], sib_recv.at[1], {"seq": sib})
     sib_k.start()
 
-    def send_half(src, dst, slot):
-        def one(r, carry):
-            d = lax.rem(q + r, chips)
-            target = core * chips + d
-
-            @pl.when(target != me)
-            def _():
-                remote(src.at[d], dst.at[q], ret_send.at[slot], ret_recv.at[slot], {"seq": target}).start()
-
-            @pl.when(target == me)
-            def _():
-                pltpu.make_async_copy(src.at[d], dst.at[q], ret_recv.at[slot]).start()
-
-            return carry
-
-        lax.fori_loop(0, chips, one, 0)
-
-    swap_k.wait()
-    own_rows = pl.ds(pl.multiple_of(core * ROWS, ROWS), half)
-    kg = (ybuf[0, pl.ds(pl.multiple_of(core * half, ROWS), half), :] + xb[0, own_rows, :]) * (1.0 / length)
-    kg_send[...] = kg.reshape(kg_send.shape)
-    send_half(kg_send, kg_ret, 0)
-
     sib_k.wait()
     forward([kbuf[...].reshape(outer, LANES)], [0])
     kr, ki = parts(0)
+    swap_c = swap(1, 3, 1)
     finish(
         [1, 2],
         [
             inverse_rows(gr * kr - gi * ki, gr * ki + gi * kr),
             inverse_rows(dr * kr + di * ki, di * kr - dr * ki),
         ],
-    )
-    swap_c = swap(1, 3, 1)
-    swap_c.start()
+        swap_c,
+    )
     swap_c.wait()
 
-    conv_out = (ybuf[1, mine, :] + xb[1]) * (1.0 / length)
-    grad_gated = (ybuf[2, mine, :] + xb[2]) * (1.0 / length)
+    conv_out = (yown[1] + xb[1]) * (1.0 / length)
+    grad_gated = (yown[2] + xb[2]) * (1.0 / length)
     lane = lax.broadcasted_iota(jnp.int32, (local, LANES), 1)
     line = lax.broadcasted_iota(jnp.int32, (local, LANES), 0)
-    is_mine = (line >= core * ROWS) & (line < core * ROWS + half)
+    is_mine = (line >= core * EXTRA) & (line < core * EXTRA + half)
     cot_all = raw[:, :, 3].astype(F32).reshape(outer, LANES)
     gp32[0:outer, :] = cot_all
     cot_mine = gp32[mine, :]
@@ -381,8 +391,30 @@
             total = total + taps[s][j] * jnp.where(lane >= LANES - j, after, turned)
         res[s] = total
         gp_send[:, s] = res[s, own_rows, :].reshape(chips, ROWS, LANES).astype(BF16)
-    send_half(gp_send, gp_ret, 1)
-
+    send_half(gp_send, gp_ret, 1, 0, chips // 2)
+
+    wait_bytes(kg_send, ret_recv.at[0])
+    weighted = env[...] * jnp.concatenate(
+        [
+            jnp.concatenate(
+                [
+                    kg_ret.at[pl.ds(cb * 8, 8)][:, j, :] for j in range(ROWS)
+                ], 1,
+            )
+            for cb in range(blocks)
+        ], 0,
+    )
+    pair = split(weighted)
+    out_part = dot3(pair, (hid2[0], hid2[1]), 1, 1)
+    grad_hidden = dot3(split(fout[...]), pair, 0, 0) * hcos[...]
+    in_part = dot3((feat2[0], feat2[1]), split(grad_hidden), 1, 1)
+    for half_at in range(2):
+        for at, part in enumerate((out_part, in_part)):
+            first = half_at * (channels // 2)
+            middle, end = first + channels // 4, first + channels // 2
+            r_own[half_at, at] = jnp.concatenate([part[first:middle], part[middle:end]], 1)
+    red_core = remote(r_own.at[1 - core], r_sib, red_send.at[0], red_recv.at[0], {"seq": sib})
+    red_core.start()
     lane1 = lax.broadcasted_iota(jnp.int32, (1, LANES), 1)
     short = jnp.zeros((1, LANES), F32)
     for s in range(3):
@@ -396,39 +428,43 @@
     sib_short = remote(s_own, s_sib, sib_send.at[2], sib_recv.at[2], {"seq": sib})
     sib_short.start()
 
+    red_core.wait()
+    r_z[zi] = r_own[core] + r_sib[...]
+
+    def to_z(r, carry):
+        device = seq_dev(xi * Z_SIZE + lax.rem(zi + r, Z_SIZE))
+        remote(r_z.at[zi], r_z.at[zi], red_send.at[1], red_recv.at[1], device).start()
+        return carry
+
+    lax.fori_loop(1, Z_SIZE, to_z, 0)
+
+
     sib_short.wait()
     s_all[q] = s_own[...] + s_sib[...]
     to_chips(
         lambda chip: remote(s_all.at[q], s_all.at[q], red_send.at[4], red_recv.at[4], seq_dev(chip)).start()
     )
-
-    wait_bytes(kg_send, ret_recv.at[0])
-    weighted = env[...] * jnp.concatenate(
-        [
-            jnp.concatenate(
-                [
-                    kg_ret.at[pl.ds(cb * 8, 8)][:, j, :] for j in range(ROWS)
-                ], 1,
-            )
-            for cb in range(blocks)
-        ], 0,
-    )
-    pair = split(weighted)
-    out_part = dot3(pair, (hid2[0], hid2[1]), 1, 1)
-    grad_hidden = dot3(split(fout[...]), pair, 0, 0) * hcos[...]
-    in_part = dot3((feat2[0], feat2[1]), split(grad_hidden), 1, 1)
-    r_own[...] = jnp.concatenate([out_part, in_part], 1).reshape(r_own.shape)
-    red_core = remote(r_own.at[1 - core], r_sib, red_send.at[0], red_recv.at[0], {"seq": sib})
-    red_core.start()
-    red_core.wait()
-    r_z[zi] = r_own[core] + r_sib[...]
-
-    def to_z(r, carry):
-        device = seq_dev(xi * Z_SIZE + lax.rem(zi + r, Z_SIZE))
-        remote(r_z.at[zi], r_z.at[zi], red_send.at[1], red_recv.at[1], device).start()
+    send_half(gp_send, gp_ret, 1, chips // 2, chips)
+
+    z_rest = r_z.at[pl.ds(0, Z_SIZE - 1)]
+    wait_bytes(z_rest, red_recv.at[1])
+    total = r_z[0]
+    for i in range(1, Z_SIZE):
+        total = total + r_z[i]
+    here = xi * y_size + yi
+    r_x[core, xi] = total[0]
+    r_xy[core, here] = total[1]
+
+    def to_cross(r, carry):
+        remote(r_xy.at[core, here], r_xy.at[core, here], red_send.at[2], red_recv.at[2], cross(r)).start()
         return carry
 
-    lax.fori_loop(1, Z_SIZE, to_z, 0)
+    def to_x(r, carry):
+        remote(r_x.at[core, xi], r_x.at[core, xi], red_send.at[3], red_recv.at[3], cross(r * y_size)).start()
+        return carry
+
+    lax.fori_loop(1, 2 * x_size * y_size, to_cross, 0)
+    lax.fori_loop(1, 2 * x_size, to_x, 0)
 
     wait_bytes(gp_send, ret_recv.at[1])
     gp32[...] = gp_ret[...].astype(F32).reshape(gp32.shape)
@@ -438,59 +474,51 @@
                 rows = pl.ds(cb * 8 * 3 * ROWS + s * ROWS + j, 8, stride=3 * ROWS)
                 gp[s, cb * 8 : cb * 8 + 8, j * LANES : (j + 1) * LANES] = gp32[rows, :].astype(BF16)
 
-    z_rest = r_z.at[pl.ds(0, Z_SIZE - 1)]
-    wait_bytes(z_rest, red_recv.at[1])
-    total = r_z[0]
-    for i in range(1, Z_SIZE):
-        total = total + r_z[i]
-    here = xi * y_size + yi
-    r_xy[here] = total
-
-    def to_cross(r, carry):
-        remote(r_xy.at[here], r_xy.at[here], red_send.at[2], red_recv.at[2], cross(r)).start()
-        return carry
-
-    lax.fori_loop(1, x_size * y_size, to_cross, 0)
-
     scale = 1.0 / math.sqrt(length)
     wait_bytes(s_all.at[pl.ds(0, chips - 1)], red_recv.at[4])
     shorts = s_all[...].reshape(channels, LANES) * scale
     for at in range(9):
-        small[channels + at : channels + at + 1, 0:channels] = as_row(shorts[:, at : at + 1])
-
-    def wait_cross(sem):
-        wait_bytes(r_xy.at[pl.ds(0, x_size * y_size - 1)], sem)
-
-    wait_cross(red_recv.at[2])
-    columns = []
-    for y in [yi] + list(range(y_size)):
-        column_sum = r_xy[y]
+        short_rows[at // 3, at % 3 : at % 3 + 1, :] = as_row(shorts[:, at : at + 1])
+
+    group = 2 * x_size * y_size
+    wait_bytes(gp32.at[pl.ds(0, (2 * x_size - 1) * (channels // 4))], red_recv.at[3])
+    wait_bytes(gp32.at[pl.ds(0, (group - 1) * (channels // 4))], red_recv.at[2])
+    for half_at in range(2):
+        out_total = r_x[half_at, 0]
         for x in range(1, x_size):
-            column_sum = column_sum + r_xy[x * y_size + y]
-        columns.append(column_sum)
-    every = columns[1]
-    for y in range(1, y_size):
-        every = every + columns[1 + y]
-    lanes = lax.broadcasted_iota(jnp.int32, every.shape, 1)
-    r_all[core] = jnp.where(lanes < units, columns[0], every) * scale
-    red_back = remote(r_all.at[core], r_all.at[core], red_send.at[3], red_recv.at[3], {"seq": sib})
-    red_back.start()
-    red_back.wait()
-    small[0:channels, :] = r_all[...].reshape(channels, LANES)
+            out_total = out_total + r_x[half_at, x]
+        in_total = r_xy[half_at, 0]
+        for at in range(1, x_size * y_size):
+            in_total = in_total + r_xy[half_at, at]
+        first = half_at * (channels // 2)
+        middle, end = first + channels // 4, first + channels // 2
+        for out, part in ((fout_out, out_total * scale), (fin_out, in_total * scale)):
+            out[first:middle, :] = part[:, :units]
+            out[middle:end, :] = part[:, units:]
 
     wait_bytes(raw_send.at[pl.ds(0, chips - 1)], in_send.at[0])
     wait_bytes(k_send.at[pl.ds(0, (chips - 1) * ROWS)], in_send.at[1])
     for slot, buf in ((0, kg_send), (1, gp_send)):
         wait_bytes(buf.at[pl.ds(0, chips - 1)], ret_send.at[slot])
 
-        @pl.when(lax.div(me, chips) != core)
+        @pl.when(jnp.logical_not(is_local))
         def _():
             wait_bytes(buf.at[0], ret_send.at[slot])
 
     wait_bytes(raw_send, sib_send.at[0])
     wait_bytes(z_rest, red_send.at[1])
-    wait_cross(red_send.at[2])
+    wait_bytes(gp32.at[pl.ds(0, (2 * x_size - 1) * (channels // 4))], red_send.at[3])
+    wait_bytes(gp32.at[pl.ds(0, (group - 1) * (channels // 4))], red_send.at[2])
     wait_bytes(s_all.at[pl.ds(0, chips - 1)], red_send.at[4])
+
+
+def move_outputs(*refs):
+    count = (len(refs) - 1) // 2
+    copies = [pltpu.make_async_copy(refs[i], refs[count + i], refs[-1].at[i]) for i in range(count)]
+    for copy in copies:
+        copy.start()
+    for copy in copies:
+        copy.wait()
 
 
 def shards(devices, y_size, tables, proj, cotangent, short_w, filter_in, filter_out, rates):
@@ -511,14 +539,17 @@
     operands = (
         proj, cotangent, short_w.transpose(0, 2, 1), filter_in, filter_out.T, rates.reshape(1, channels), *tables
     )
-    grad_proj, small = pl.pallas_call(
+    shapes = (
+        jax.ShapeDtypeStruct(proj.shape, BF16),
+        jax.ShapeDtypeStruct((3, 3, channels), F32),
+        jax.ShapeDtypeStruct((channels, order), F32),
+        jax.ShapeDtypeStruct((feats, order), F32),
+    )
+    results = pl.pallas_call(
         functools.partial(kernel, devices, y_size),
-        out_shape=(
-            jax.ShapeDtypeStruct(proj.shape, BF16),
-            jax.ShapeDtypeStruct((channels + 16, LANES), F32),
-        ),
+        out_shape=shapes,
         in_specs=[hbm] * 11,
-        out_specs=(pl.BlockSpec(memory_space=pltpu.VMEM),) * 2,
+        out_specs=(pl.BlockSpec(memory_space=pltpu.VMEM),) * 4,
         scratch_shapes=[
             bf16(*proj.shape),
             bf16(*cotangent.shape),
@@ -527,7 +558,7 @@
             f32(channels, order),
             f32(1, channels),
             bf16(2, outer, outer),
-            bf16(2, outer, outer),
+            bf16(2, outer + 2 * EXTRA, outer),
             f32(2, half, LANES),
             bf16(2, 2 * LANES, 2 * LANES),
             bf16(2, 2 * LANES, 2 * LANES),
@@ -542,21 +573,22 @@
             f32(3, 2, outer, LANES),
             f32(2, outer, LANES),
             f32(3, half, 2 * LANES),
-            f32(3, outer, LANES),
-            f32(3, half + ROWS, LANES),
+            f32(3, half + EXTRA, LANES),
+            f32(3, half + EXTRA, LANES),
+            f32(3, half + EXTRA, LANES),
             f32(chips, ROWS, LANES),
             f32(chips, ROWS, LANES),
-            f32(3, half + ROWS, LANES),
+            f32(3, half + EXTRA, LANES),
             bf16(chips, 3, ROWS, LANES),
             bf16(chips, 3, ROWS, LANES),
             f32(chips * 3 * ROWS, LANES),
             bf16(2, order, TOKENS),
             bf16(2, feats, TOKENS),
-            f32(2, channels // 2, LANES),
-            f32(channels // 2, LANES),
-            f32(Z_SIZE, channels // 2, LANES),
-            f32(chips // Z_SIZE * y_size, channels // 2, LANES),
-            f32(2, channels // 2, LANES),
+            f32(2, 2, channels // 4, LANES),
+            f32(2, channels // 4, LANES),
+            f32(Z_SIZE, 2, channels // 4, LANES),
+            f32(2, chips // Z_SIZE, channels // 4, LANES),
+            f32(2, chips // Z_SIZE * y_size, channels // 4, LANES),
             f32(1, LANES),
             f32(1, LANES),
             f32(chips, 1, LANES),
@@ -567,8 +599,15 @@
             collective_id=0, has_side_effects=True, vmem_limit_bytes=32 << 20
         ),
     )(*[pltpu.with_memory_space_constraint(x, pltpu.HBM) for x in operands])
-    grad_short = small[channels : channels + 9, :channels].reshape(3, 3, channels).transpose(0, 2, 1)
-    return grad_proj, grad_short, small[:channels, :order].T, small[:feats, order:]
+    grad_proj, grad_short, grad_out, grad_in = pl.pallas_call(
+        move_outputs,
+        out_shape=shapes,
+        in_specs=[pl.BlockSpec(memory_space=pl.ANY)] * 4,
+        out_specs=(hbm,) * 4,
+        scratch_shapes=[dma((4,))],
+        compiler_params=pltpu.CompilerParams(vmem_limit_bytes=1 << 20),
+    )(*results)
+    return grad_proj, grad_short.transpose(0, 2, 1), grad_out.T, grad_in
 
 
 def solution(mesh):

time: 51 us -> 46.9 us (0.920)
  Pallas kernels: 48.3 us -> 46.1 us
  local copies, waits for them, and re-layouts: 1.96 us -> 0 us
    pallas_call x1 -> x2, Pallas kernels: 48.3 us -> 46.1 us  [the longest x1 45.4 us: shards(): pl.pallas_call(functools.partial(kernel, devices, y_size), out_shape=shap...]
    slice x2 -> x0, local copies, waits for them, and re-layouts: 0.68 us -> none  [the longest x1 0.68 us: shards(): small[:feats, order:]]
    unnamed x1 -> x0, local copies, waits for them, and re-layouts: 0.68 us -> none
    reshape x1 -> x0, local copies, waits for them, and re-layouts: 0.6 us -> none  [shards(): small[channels:channels + 9, :channels].reshape(3, 3, channels)]
where the time goes in v5:
time: 46.9 us; the launch traced here: 46.8 us
  Pallas kernels  46.1 us (98%)
  between operations  0.64 us (1%)
    pallas_call x1, Pallas kernels, shards(): pl.pallas_call(functools.partial(kernel, devices, y_size), out_shape=shap...  45.4 us

profile of v5, /device:TPU:1, one launch (start us, length us, event | category | flops | bytes accessed | tf_op | source)
XLA Modules:
  0.0 46.8 jit_solution(9962930491183388846)
XLA Ops:
  0.6 45.4 %shard_map.138 = (bf16[3,32,1024]{2,1,0:T(8,128)(2,1)S(1)}, f32[3,3,32]{2,1,0:T(4,128)S(1)}, f32[32,64]{1,0:T(8,128)S(1)}, f32[32,64]{1,0:T(8,128)S(1)}) custom-call(bf16[3,32,1024]{2,1,0:T(8,128)(2,1)} %proj_hbm.1, bf16[32,1024]{1,0:T(8,128)(2,1)} %cot_hbm.1, f32[3,3,32]{2,1,0:T(4,128)} %bitcast.6, f32[32,64]{1,0:T(8,128)} %fin_hbm.1, f32[32,64]{1,0:T(8,128)} %bitcast.5, ...), custom_call_target="tpu_custom_call" | custom-call | tf_op jit(solution)/shard_map/pallas_call | solution.py:548
  46.1 0.7 %shard_map.139 = (bf16[3,32,1024]{2,1,0:T(8,128)(2,1)}, f32[3,3,32]{2,1,0:T(4,128)}, f32[32,64]{1,0:T(8,128)}, f32[32,64]{1,0:T(8,128)}) custom-call(bf16[3,32,1024]{2,1,0:T(8,128)(2,1)S(1)} %get-tuple-element.12.refs_0_, f32[3,3,32]{2,1,0:T(4,128)S(1)} %get-tuple-element.13.refs_1_, f32[32,64]{1,0:T(8,128)S(1)} %get-tuple-element.14.refs_2_, ...), custom_call_target="tpu_custom_call" | custom-call | tf_op jit(solution)/shard_map/pallas_call | solution.py:602

commit v6 on v5

--- a/solution.py
+++ b/solution.py
@@ -169,15 +169,24 @@
         other = lax.rem(core + lax.div(r, x_size * y_size), 2)
         return {"ch": lax.rem(yi + lax.rem(r, y_size), y_size), "seq": 2 * (x * Z_SIZE + zi) + other}
 
-    def greet(r, carry):
-        pl.semaphore_signal(barrier, inc=1, device_id=seq_dev(lax.rem(q + r, chips)), device_id_type=MESH)
-        return carry
+    def ring_offset(k):
+        return Z_SIZE // 2 + jnp.where(lax.rem(k, 2) == 1, -lax.div(k + 1, 2), lax.div(k, 2))
 
     def greet_cross(r, carry):
         pl.semaphore_signal(barrier, inc=1, device_id=cross(r), device_id_type=MESH)
         return carry
 
-    lax.fori_loop(1, chips, greet, 0)
+    def greet_far(k, carry):
+        z = lax.rem(zi + ring_offset(k), Z_SIZE)
+        for dx in (2, 1, 3, 0):
+            chip = lax.rem(xi + dx, x_size) * Z_SIZE + z
+            pl.semaphore_signal(barrier, inc=1, device_id=seq_dev(chip), device_id_type=MESH)
+        return carry
+
+    lax.fori_loop(0, Z_SIZE - 1, greet_far, 0)
+    for dx in range(1, x_size):
+        chip = lax.rem(xi + dx, x_size) * Z_SIZE + zi
+        pl.semaphore_signal(barrier, inc=1, device_id=seq_dev(chip), device_id_type=MESH)
     lax.fori_loop(1, 2 * x_size * y_size, greet_cross, 0)
     for i in order:
         loads[i].start()
@@ -353,7 +362,32 @@
     own_rows = pl.ds(pl.multiple_of(core * EXTRA, ROWS), half)
     kg = (yown[0, own_rows, :] + xb[0, own_rows, :]) * (1.0 / length)
     kg_send[...] = kg.reshape(kg_send.shape)
-    send_half(kg_send, kg_ret, 0, 0, chips)
+
+    def kg_push(d):
+        device = {"seq": core * chips + d}
+        remote(kg_send.at[d], kg_ret.at[q], ret_send.at[0], ret_recv.at[0], device).start()
+
+    def kg_blocks(k):
+        z = lax.rem(zi + ring_offset(k), Z_SIZE)
+        return [x * 2 * Z_SIZE + 2 * z + c for x in range(x_size // 2) for c in range(2)]
+
+    def kg_far(k, carry):
+        for d in kg_blocks(k):
+            kg_push(d)
+        return carry
+
+    lax.fori_loop(0, Z_SIZE - 1, kg_far, 0)
+    for d in kg_blocks(jnp.int32(Z_SIZE - 1)):
+        is_me = core * chips + d == me
+
+        @pl.when(is_me)
+        def _():
+            pltpu.make_async_copy(kg_send.at[d], kg_ret.at[q], ret_recv.at[0]).start()
+
+        @pl.when(jnp.logical_not(is_me))
+        def _():
+            kg_push(d)
+
 
     wait_bytes(k_send.at[pl.ds(0, (chips - 1) * ROWS)], in_recv.at[1])
     sib_k = remote(kbuf.at[:, core], kbuf.at[:, core], sib_send.at[1], sib_recv.at[1], {"seq": sib})

time: 46.9 us -> 46 us (0.981)
  Pallas kernels: 46.1 us -> 45.3 us
    pallas_call x1, Pallas kernels: 45.4 us -> 44.6 us  [shards(): pl.pallas_call(functools.partial(kernel, devices, y_size), out_shape=shap...]
where the time goes in v6:
time: 46 us; the launch traced here: 45.9 us
  Pallas kernels  45.3 us (98%)
  between operations  0.64 us (1%)
    pallas_call x1, Pallas kernels, shards(): pl.pallas_call(functools.partial(kernel, devices, y_size), out_shape=shap...  44.6 us

profile of v6, /device:TPU:1, one launch (start us, length us, event | category | flops | bytes accessed | tf_op | source)
XLA Modules:
  0.0 45.9 jit_solution(11403050941808217118)
XLA Ops:
  0.6 44.6 %shard_map.138 = (bf16[3,32,1024]{2,1,0:T(8,128)(2,1)S(1)}, f32[3,3,32]{2,1,0:T(4,128)S(1)}, f32[32,64]{1,0:T(8,128)S(1)}, f32[32,64]{1,0:T(8,128)S(1)}) custom-call(bf16[3,32,1024]{2,1,0:T(8,128)(2,1)} %proj_hbm.1, bf16[32,1024]{1,0:T(8,128)(2,1)} %cot_hbm.1, f32[3,3,32]{2,1,0:T(4,128)} %bitcast.6, f32[32,64]{1,0:T(8,128)} %fin_hbm.1, f32[32,64]{1,0:T(8,128)} %bitcast.5, ...), custom_call_target="tpu_custom_call" | custom-call | tf_op jit(solution)/shard_map/pallas_call | solution.py:582
  45.2 0.7 %shard_map.139 = (bf16[3,32,1024]{2,1,0:T(8,128)(2,1)}, f32[3,3,32]{2,1,0:T(4,128)}, f32[32,64]{1,0:T(8,128)}, f32[32,64]{1,0:T(8,128)}) custom-call(bf16[3,32,1024]{2,1,0:T(8,128)(2,1)S(1)} %get-tuple-element.12.refs_0_, f32[3,3,32]{2,1,0:T(4,128)S(1)} %get-tuple-element.13.refs_1_, f32[32,64]{1,0:T(8,128)S(1)} %get-tuple-element.14.refs_2_, ...), custom_call_target="tpu_custom_call" | custom-call | tf_op jit(solution)/shard_map/pallas_call | solution.py:636

commit v7 on v6

--- a/solution.py
+++ b/solution.py
@@ -216,17 +216,20 @@
         return pl.ds(pl.multiple_of(chip * ROWS, ROWS), ROWS)
 
     def to_chips(start):
-        def one(r, carry):
-            start(lax.rem(q + r, chips))
+        def far(k, carry):
+            z = lax.rem(zi + ring_offset(k), Z_SIZE)
+            for dx in (2, 1, 3, 0):
+                start(lax.rem(xi + dx, x_size) * Z_SIZE + z)
             return carry
 
-        lax.fori_loop(1, chips, one, 0)
-
-    to_chips(
-        lambda chip: remote(
-            raw_send.at[chip], raw.at[q, core], in_send.at[0], raw_recv.at[q], seq_dev(chip)
-        ).start()
-    )
+        lax.fori_loop(0, Z_SIZE - 1, far, 0)
+        for dx in (2, 1, 3):
+            start(lax.rem(xi + dx, x_size) * Z_SIZE + zi)
+
+    def send_raw(chip):
+        remote(raw_send.at[chip], raw.at[q, core], in_send.at[0], raw_recv.at[q], seq_dev(chip)).start()
+
+    to_chips(send_raw)
     raw[q, core] = raw_send[q]
 
     row = lax.broadcasted_iota(jnp.int32, feat.shape, 0)
@@ -262,21 +265,27 @@
     def hand_on(chip):
         remote(raw.at[chip, core], raw.at[chip, core], sib_send.at[0], sib_recv.at[0], {"seq": sib}).start()
 
-    def arrived(r, carry):
-        chip = lax.rem(q + chips - r, chips)
+    def arrived(chip):
         pltpu.make_async_copy(raw.at[chip, core], raw.at[chip, core], raw_recv.at[chip]).wait()
         hand_on(chip)
+
+    def arrived_far(k, carry):
+        z = lax.rem(zi + Z_SIZE - ring_offset(k), Z_SIZE)
+        for dx in (2, 3, 1, 0):
+            arrived(lax.rem(xi + dx, x_size) * Z_SIZE + z)
         return carry
 
     hand_on(q)
-    lax.fori_loop(1, chips // 2, arrived, 0)
+    lax.fori_loop(0, Z_SIZE // 2, arrived_far, 0)
     to_chips(
         lambda chip: remote(
             k_send.at[rows_of(chip)], kbuf.at[q, core], in_send.at[1], in_recv.at[1], seq_dev(chip)
         ).start()
     )
     kbuf[q, core] = k_send[rows_of(q)]
-    lax.fori_loop(chips // 2, chips, arrived, 0)
+    lax.fori_loop(Z_SIZE // 2, Z_SIZE - 1, arrived_far, 0)
+    for dx in (2, 3, 1):
+        arrived(lax.rem(xi + dx, x_size) * Z_SIZE + zi)
     wait_bytes(raw_send, sib_recv.at[0])
 
     lane = lax.broadcasted_iota(jnp.int32, (outer, LANES), 1)
@@ -298,12 +307,19 @@
     grad_conv = raw[:, :, 3].astype(F32).reshape(outer, LANES) * mixed[0]
 
     def forward(values, slots):
-        u = dot3((f1[0], f1[1]), split(jnp.concatenate(values, 1) if len(values) > 1 else values[0]))
-        for at, s in enumerate(slots):
-            ur = u[:half, at * LANES : (at + 1) * LANES]
-            ui = u[half:, at * LANES : (at + 1) * LANES]
-            v = jnp.concatenate([ur * tw[0] - ui * tw[1], ur * tw[1] + ui * tw[0]], 1)
-            spec[s] = dot3(split(v), (f2[0], f2[1]))
+        right = split(jnp.concatenate(values, 1) if len(values) > 1 else values[0])
+        step = half // 4
+        for first in range(0, half, step):
+            ours = slice(first, first + step)
+            rows = (ours, slice(half + first, half + first + step))
+            left = [jnp.concatenate([f1[part, r, :] for r in rows], 0) for part in range(2)]
+            u = dot3(left, right)
+            for at, s in enumerate(slots):
+                ur = u[:step, at * LANES : (at + 1) * LANES]
+                ui = u[step:, at * LANES : (at + 1) * LANES]
+                tr, ti = tw[0, ours, :], tw[1, ours, :]
+                v = jnp.concatenate([ur * tr - ui * ti, ur * ti + ui * tr], 1)
+                spec[s, ours, :] = dot3(split(v), (f2[0], f2[1]))
 
     def parts(s):
         return spec[s, :, :LANES], spec[s, :, LANES:]
@@ -465,13 +481,9 @@
     red_core.wait()
     r_z[zi] = r_own[core] + r_sib[...]
 
-    def to_z(r, carry):
-        device = seq_dev(xi * Z_SIZE + lax.rem(zi + r, Z_SIZE))
+    for dz in (4, 3, 5, 2, 6, 1, 7):
+        device = seq_dev(xi * Z_SIZE + lax.rem(zi + dz, Z_SIZE))
         remote(r_z.at[zi], r_z.at[zi], red_send.at[1], red_recv.at[1], device).start()
-        return carry
-
-    lax.fori_loop(1, Z_SIZE, to_z, 0)
-
 
     sib_short.wait()
     s_all[q] = s_own[...] + s_sib[...]
@@ -489,16 +501,29 @@
     r_x[core, xi] = total[0]
     r_xy[core, here] = total[1]
 
-    def to_cross(r, carry):
-        remote(r_xy.at[core, here], r_xy.at[core, here], red_send.at[2], red_recv.at[2], cross(r)).start()
+    def around(dx, dy, other):
+        x = lax.rem(xi + dx, x_size)
+        return {"ch": lax.rem(yi + dy, y_size), "seq": 2 * (x * Z_SIZE + zi) + (1 - core if other else core)}
+
+    def sum_in(dx, dy, other):
+        remote(
+            r_xy.at[core, here], r_xy.at[core, here], red_send.at[2], red_recv.at[2], around(dx, dy, other)
+        ).start()
+
+    def sum_in_far(k, carry):
+        dx = 2 + jnp.where(k == 0, 0, jnp.where(k == 1, -1, 1))
+        for other in (True, False):
+            for dy in (2, 1, 3, 0):
+                sum_in(dx, dy, other)
         return carry
 
-    def to_x(r, carry):
-        remote(r_x.at[core, xi], r_x.at[core, xi], red_send.at[3], red_recv.at[3], cross(r * y_size)).start()
-        return carry
-
-    lax.fori_loop(1, 2 * x_size * y_size, to_cross, 0)
-    lax.fori_loop(1, 2 * x_size, to_x, 0)
+    lax.fori_loop(0, x_size - 1, sum_in_far, 0)
+    for dy, other in ((2, True), (2, False), (1, True), (3, True), (1, False), (3, False), (0, True)):
+        sum_in(0, dy, other)
+    for dx, other in ((2, True), (2, False), (1, True), (3, True), (1, False), (3, False), (0, True)):
+        remote(
+            r_x.at[core, xi], r_x.at[core, xi], red_send.at[3], red_recv.at[3], around(dx, 0, other)
+        ).start()
 
     wait_bytes(gp_send, ret_recv.at[1])
     gp32[...] = gp_ret[...].astype(F32).reshape(gp32.shape)

time: 46 us -> 44.9 us (0.976)
  Pallas kernels: 45.3 us -> 44.1 us
    pallas_call x1, Pallas kernels: 44.6 us -> 43.4 us  [shards(): pl.pallas_call(functools.partial(kernel, devices, y_size), out_shape=shap...]
where the time goes in v7:
time: 44.9 us; the launch traced here: 44.8 us
  Pallas kernels  44.1 us (98%)
  between operations  0.64 us (1%)
    pallas_call x1, Pallas kernels, shards(): pl.pallas_call(functools.partial(kernel, devices, y_size), out_shape=shap...  43.4 us

profile of v7, /device:TPU:1, one launch (start us, length us, event | category | flops | bytes accessed | tf_op | source)
XLA Modules:
  0.0 44.8 jit_solution(9917001842258713425)
XLA Ops:
  0.6 43.4 %shard_map.138 = (bf16[3,32,1024]{2,1,0:T(8,128)(2,1)S(1)}, f32[3,3,32]{2,1,0:T(4,128)S(1)}, f32[32,64]{1,0:T(8,128)S(1)}, f32[32,64]{1,0:T(8,128)S(1)}) custom-call(bf16[3,32,1024]{2,1,0:T(8,128)(2,1)} %proj_hbm.1, bf16[32,1024]{1,0:T(8,128)(2,1)} %cot_hbm.1, f32[3,3,32]{2,1,0:T(4,128)} %bitcast.6, f32[32,64]{1,0:T(8,128)} %fin_hbm.1, f32[32,64]{1,0:T(8,128)} %bitcast.5, ...), custom_call_target="tpu_custom_call" | custom-call | tf_op jit(solution)/shard_map/pallas_call | solution.py:607
  44.1 0.7 %shard_map.139 = (bf16[3,32,1024]{2,1,0:T(8,128)(2,1)}, f32[3,3,32]{2,1,0:T(4,128)}, f32[32,64]{1,0:T(8,128)}, f32[32,64]{1,0:T(8,128)}) custom-call(bf16[3,32,1024]{2,1,0:T(8,128)(2,1)S(1)} %get-tuple-element.12.refs_0_, f32[3,3,32]{2,1,0:T(4,128)S(1)} %get-tuple-element.13.refs_1_, f32[32,64]{1,0:T(8,128)S(1)} %get-tuple-element.14.refs_2_, ...), custom_call_target="tpu_custom_call" | custom-call | tf_op jit(solution)/shard_map/pallas_call | solution.py:661

commit v8 on v7

--- a/solution.py
+++ b/solution.py
@@ -164,17 +164,24 @@
     xi = lax.div(q, Z_SIZE)
     zi = lax.rem(q, Z_SIZE)
 
-    def cross(r):
-        x = lax.rem(xi + lax.rem(lax.div(r, y_size), x_size), x_size)
-        other = lax.rem(core + lax.div(r, x_size * y_size), 2)
-        return {"ch": lax.rem(yi + lax.rem(r, y_size), y_size), "seq": 2 * (x * Z_SIZE + zi) + other}
+    def around(dx, dy, other):
+        x = lax.rem(xi + dx, x_size)
+        return {"ch": lax.rem(yi + dy, y_size), "seq": 2 * (x * Z_SIZE + zi) + (1 - core if other else core)}
 
     def ring_offset(k):
         return Z_SIZE // 2 + jnp.where(lax.rem(k, 2) == 1, -lax.div(k + 1, 2), lax.div(k, 2))
 
-    def greet_cross(r, carry):
-        pl.semaphore_signal(barrier, inc=1, device_id=cross(r), device_id_type=MESH)
-        return carry
+    def over_group(act):
+        def far(k, carry):
+            dx = 2 + jnp.where(k == 0, 0, jnp.where(k == 1, -1, 1))
+            for other in (True, False):
+                for dy in (2, 1, 3, 0):
+                    act(dx, dy, other)
+            return carry
+
+        lax.fori_loop(0, x_size - 1, far, 0)
+        for dy, other in ((2, True), (2, False), (1, True), (3, True), (1, False), (3, False), (0, True)):
+            act(0, dy, other)
 
     def greet_far(k, carry):
         z = lax.rem(zi + ring_offset(k), Z_SIZE)
@@ -183,12 +190,18 @@
             pl.semaphore_signal(barrier, inc=1, device_id=seq_dev(chip), device_id_type=MESH)
         return carry
 
+    for i in order[:2]:
+        loads[i].start()
     lax.fori_loop(0, Z_SIZE - 1, greet_far, 0)
     for dx in range(1, x_size):
         chip = lax.rem(xi + dx, x_size) * Z_SIZE + zi
         pl.semaphore_signal(barrier, inc=1, device_id=seq_dev(chip), device_id_type=MESH)
-    lax.fori_loop(1, 2 * x_size * y_size, greet_cross, 0)
-    for i in order:
+    over_group(
+        lambda dx, dy, other: pl.semaphore_signal(
+            barrier, inc=1, device_id=around(dx, dy, other), device_id_type=MESH
+        )
+    )
+    for i in order[2:]:
         loads[i].start()
 
     def remote(src, dst, send_sem, recv_sem, device):
@@ -276,14 +289,14 @@
         return carry
 
     hand_on(q)
-    lax.fori_loop(0, Z_SIZE // 2, arrived_far, 0)
+    lax.fori_loop(0, Z_SIZE - 2, arrived_far, 0)
     to_chips(
         lambda chip: remote(
             k_send.at[rows_of(chip)], kbuf.at[q, core], in_send.at[1], in_recv.at[1], seq_dev(chip)
         ).start()
     )
     kbuf[q, core] = k_send[rows_of(q)]
-    lax.fori_loop(Z_SIZE // 2, Z_SIZE - 1, arrived_far, 0)
+    lax.fori_loop(Z_SIZE - 2, Z_SIZE - 1, arrived_far, 0)
     for dx in (2, 3, 1):
         arrived(lax.rem(xi + dx, x_size) * Z_SIZE + zi)
     wait_bytes(raw_send, sib_recv.at[0])
@@ -501,25 +514,12 @@
     r_x[core, xi] = total[0]
     r_xy[core, here] = total[1]
 
-    def around(dx, dy, other):
-        x = lax.rem(xi + dx, x_size)
-        return {"ch": lax.rem(yi + dy, y_size), "seq": 2 * (x * Z_SIZE + zi) + (1 - core if other else core)}
-
     def sum_in(dx, dy, other):
         remote(
             r_xy.at[core, here], r_xy.at[core, here], red_send.at[2], red_recv.at[2], around(dx, dy, other)
         ).start()
 
-    def sum_in_far(k, carry):
-        dx = 2 + jnp.where(k == 0, 0, jnp.where(k == 1, -1, 1))
-        for other in (True, False):
-            for dy in (2, 1, 3, 0):
-                sum_in(dx, dy, other)
-        return carry
-
-    lax.fori_loop(0, x_size - 1, sum_in_far, 0)
-    for dy, other in ((2, True), (2, False), (1, True), (3, True), (1, False), (3, False), (0, True)):
-        sum_in(0, dy, other)
+    over_group(sum_in)
     for dx, other in ((2, True), (2, False), (1, True), (3, True), (1, False), (3, False), (0, True)):
         remote(
             r_x.at[core, xi], r_x.at[core, xi], red_send.at[3], red_recv.at[3], around(dx, 0, other)

time: 44.9 us -> 44.9 us (level)
  no operation moved by 1% of the time
where the time goes in v8:
time: 44.9 us; the launch traced here: 44.8 us
  Pallas kernels  44.1 us (98%)
  between operations  0.64 us (1%)
    pallas_call x1, Pallas kernels, shards(): pl.pallas_call(functools.partial(kernel, devices, y_size), out_shape=shap...  43.4 us

profile of v8, /device:TPU:1, one launch (start us, length us, event | category | flops | bytes accessed | tf_op | source)
XLA Modules:
  0.0 44.8 jit_solution(16988823090196957460)
XLA Ops:
  0.6 43.4 %shard_map.138 = (bf16[3,32,1024]{2,1,0:T(8,128)(2,1)S(1)}, f32[3,3,32]{2,1,0:T(4,128)S(1)}, f32[32,64]{1,0:T(8,128)S(1)}, f32[32,64]{1,0:T(8,128)S(1)}) custom-call(bf16[3,32,1024]{2,1,0:T(8,128)(2,1)} %proj_hbm.1, bf16[32,1024]{1,0:T(8,128)(2,1)} %cot_hbm.1, f32[3,3,32]{2,1,0:T(4,128)} %bitcast.6, f32[32,64]{1,0:T(8,128)} %fin_hbm.1, f32[32,64]{1,0:T(8,128)} %bitcast.5, ...), custom_call_target="tpu_custom_call" | custom-call | tf_op jit(solution)/shard_map/pallas_call | solution.py:607
  44.0 0.7 %shard_map.139 = (bf16[3,32,1024]{2,1,0:T(8,128)(2,1)}, f32[3,3,32]{2,1,0:T(4,128)}, f32[32,64]{1,0:T(8,128)}, f32[32,64]{1,0:T(8,128)}) custom-call(bf16[3,32,1024]{2,1,0:T(8,128)(2,1)S(1)} %get-tuple-element.12.refs_0_, f32[3,3,32]{2,1,0:T(4,128)S(1)} %get-tuple-element.13.refs_1_, f32[32,64]{1,0:T(8,128)S(1)} %get-tuple-element.14.refs_2_, ...), custom_call_target="tpu_custom_call" | custom-call | tf_op jit(solution)/shard_map/pallas_call | solution.py:661
